TPU v7x, 32 devices: a whole 2x2x4 slice. The times are simulated.
32 devices in a mesh: node: 2 (over core), dp: 16 (over z, y, x).
Axes of the slice: x: 2, y: 2, z: 4, core: 2. Of those that a mesh axis runs over, the one named last changes fastest.
Arguments:
- hidden: bfloat16 [16, 256, 13824], P('dp', 'node'), may hold values from -6 to 6
- cotangent: bfloat16 [16, 256, 16], P('dp', 'node'), may hold values from -0.375 to 0.375
- momentum: float32 [16, 16, 13824], P('dp', 'node'), may hold values from -6 to 6
- worker_error: float32 [16, 16, 13824], P('dp', 'node'), may hold values from -1.8 to 1.8
- server_error: float32 [16, 13824], P('node', 'dp'), may hold values from -0.3 to 0.3
- master: float32 [16, 13824], P('node'), may hold values from -3 to 3
- second_moment: float32 [16, 13824], P('node'), may hold values from 0.0004 to 0.01
Outputs:
- moment: float32 [16, 16, 13824], P('dp', 'node')
- new_worker_error: float32 [16, 16, 13824], P('dp', 'node')
- new_server_error: float32 [16, 13824], P('node', 'dp')
- weights: bfloat16 [16, 13824], replicated
All inputs are finite; a program needn't handle non-finite values.
Results may differ from a plain program's by a relative error of at most 0.0085.
Values may be sent and summed in bfloat16 or wider, within the bound.
No kernel may reach another device: no remote copies, remote signals or barrier semaphores. Data moves between devices by JAX's collectives and lax.ppermute only.
A program may use at most 64 MiB of HBM per device.

v0:
```python
import jax
import jax.numpy as jnp
from jax import lax
from jax.sharding import PartitionSpec as P

beta_one = 0.9
epsilon = 1e-06
learn_rate = 0.5


def body(hidden, cotangent, momentum, worker_error, server_error, master, second_moment):
    local_acts = hidden[0]
    local_cotan = cotangent[0]
    half_cols = local_acts.shape[1] // 2

    def half_sum(acts_half):
        return lax.psum_scatter(
            jnp.einsum("tc,tf->cf", local_cotan, acts_half, preferred_element_type=jnp.float32),
            "node",
            scatter_dimension=0,
            tiled=True,
        )

    first_half = half_sum(local_acts[:, :half_cols])
    second_half = half_sum(local_acts[:, half_cols:])
    gradient = jnp.concatenate([first_half, second_half], axis=1)
    moment = beta_one * momentum[0] + (1.0 - beta_one) * gradient
    carried = moment + worker_error[0]
    worker_scale = jnp.sqrt(jnp.mean(carried * carried) + epsilon)
    outgoing = (worker_scale * jnp.tanh(carried / worker_scale)).astype(jnp.bfloat16)
    new_worker = carried - outgoing.astype(jnp.float32)
    replicas = lax.axis_size("dp")
    arrived = lax.all_to_all(outgoing[None], "dp", split_axis=2, concat_axis=0, tiled=True)
    served = jnp.sum(arrived.astype(jnp.float32), axis=0) / replicas + server_error
    server_scale = jnp.sqrt(jnp.mean(served * served) + epsilon)
    returned = (server_scale * jnp.tanh(served / server_scale)).astype(jnp.bfloat16)
    new_server = served - returned.astype(jnp.float32)
    averaged = lax.all_gather(returned, "dp", axis=1, tiled=True)
    update = averaged.astype(jnp.float32) / (jnp.sqrt(second_moment) + 1e-08)
    weight_part = (master - learn_rate * update).astype(jnp.bfloat16)
    weights = lax.all_gather(weight_part, "node", axis=0, tiled=True)
    return (moment[None], new_worker[None], new_server, weights)


def solution(mesh):
    placed = (
        P("dp", "node", None),
        P("dp", "node", None),
        P("dp", "node", None),
        P("dp", "node", None),
        P("node", "dp"),
        P("node", None),
        P("node", None),
    )
    return jax.shard_map(
        body,
        mesh=mesh,
        in_specs=placed,
        out_specs=(P("dp", "node", None), P("dp", "node", None), P("node", "dp"), P()),
        check_vma=False,
    )
```

profile of v0, /device:TPU:0, one launch (start us, length us, event | category | flops | bytes accessed | tf_op | source)
XLA Modules:
  0.0 220.5 jit_solution(16023179582607611610)
XLA Ops:
  7.2 0.0 copy-start
  7.2 0.0 copy-start.1
  7.2 0.0 reduce-scatter.3.cloned.1.call-start
  7.2 0.6 copy-done
  7.9 2.6 %fusion.2 = f32[16,6912]{1,0:T(8,128)} fusion(bf16[128,13824]{1,0:T(8,128)(2,1)} %bitcast.32, bf16[1,128,16]{1,2,0:T(8,128)(2,1)S(1)} %copy-done), kind=kOutput, calls=%fused_computation.2 | convolution fusion | flops 28311552 | bytes 2215936 | tf_op jit(solution)/shard_map/tc,tf->cf/dot_general | solution.py:18
  10.4 0.0 reduce-scatter.3.cloned.1.call-update
  10.5 0.0 reduce-scatter.5.cloned.1.call-start
  10.5 2.6 %fusion = f32[16,6912]{1,0:T(8,128)} fusion(bf16[128,13824]{1,0:T(8,128)(2,1)} %bitcast.33, bf16[1,128,16]{1,2,0:T(8,128)(2,1)S(1)} %copy-done), kind=kOutput, calls=%fused_computation | convolution fusion | flops 28311552 | bytes 2215936 | tf_op jit(solution)/shard_map/tc,tf->cf/dot_general | solution.py:18
  13.1 0.0 reduce-scatter.5.cloned.1.call-update
  13.1 8.3 %reduce-scatter.3.cloned.1.call-done = f32[8,6912]{1,0:T(8,128)} async-done(((f32[16,6912]{1,0:T(8,128)}), f32[8,6912]{1,0:T(8,128)}) %reduce-scatter.3.cloned.1.call-update) | async-done | bytes 221200 | tf_op jit(solution)/shard_map/reduce_scatter | solution.py:17
  21.4 11.8 %reduce-scatter.5.cloned.1.call-done = f32[8,6912]{1,0:T(8,128)} async-done(((f32[16,6912]{1,0:T(8,128)}), f32[8,6912]{1,0:T(8,128)}) %reduce-scatter.5.cloned.1.call-update) | async-done | bytes 221200 | tf_op jit(solution)/shard_map/reduce_scatter | solution.py:17
  33.3 1.8 fusion.8
  35.8 1.9 multiply_convert_fusion
  37.7 10.7 %copy.20 = bf16[1,8,13824]{1,0,2:T(2,128)(2,1)} copy(bf16[1,8,13824]{2,1,0:T(8,128)(2,1)S(1)} %get-tuple-element.8) | data formatting | bytes 442368 | tf_op jit(solution)/shard_map/convert_element_type | solution.py:30
  48.4 0.5 broadcast.19
  48.9 75.3 %reduce.3 = bf16[13824,8]{1,0:T(8,128)(2,1)S(1)} reduce(bf16[13824,1,8]{2,1,0:T(2,128)(2,1)} %bitcast.31, bf16[]{:T(256)} %broadcast.19), dimensions={1}, to_apply=%bitcast.27.reduce_sub_computation | reduce | bytes 442370
  124.2 4.5 %reshape.51 = bf16[16,2,3456]{2,1,0:T(2,128)(2,1)} reshape(bf16[13824,8]{1,0:T(8,128)(2,1)S(1)} %reduce.3) | data formatting | bytes 442368
  128.8 6.7 %all-to-all-start = ((bf16[16,2,3456]{2,1,0:T(2,128)(2,1)}), bf16[16,2,3456]{2,1,0:T(2,128)(2,1)S(1)}, u32[]{:S(2)}, u32[]{:S(2)}) async-start(bf16[16,2,3456]{2,1,0:T(2,128)(2,1)} %reshape.51), calls=%async_computation.2 | async-start | bytes 442368 | tf_op jit(solution)/shard_map/all_to_all | solution.py:33
  135.5 2.0 convert_subtract_fusion
  137.6 7.6 %all-to-all-done = bf16[16,2,3456]{2,1,0:T(2,128)(2,1)S(1)} async-done(((bf16[16,2,3456]{2,1,0:T(2,128)(2,1)}), bf16[16,2,3456]{2,1,0:T(2,128)(2,1)S(1)}, u32[]{:S(2)}, u32[]{:S(2)}) %all-to-all-start) | async-done | bytes 221216 | tf_op jit(solution)/shard_map/all_to_all | solution.py:33
  145.1 11.2 %reshape.52 = bf16[13824,1,8]{2,1,0:T(2,128)(2,1)} reshape(bf16[16,2,3456]{2,1,0:T(2,128)(2,1)S(1)} %all-to-all-done) | data formatting | bytes 442368
  156.3 9.5 %bitcast_convert_fusion = f32[1,8,13824]{1,0,2:T(1,128)} fusion(bf16[13824,1,8]{2,1,0:T(2,128)(2,1)} %reshape.52), kind=kLoop, calls=%fused_computation.24 | loop fusion | flops 110592 | bytes 663552 | tf_op jit(solution)/shard_map/convert_element_type | solution.py:34
  165.8 0.0 copy-start.4
  165.9 3.6 %reduce_sum.28 = f32[8,864]{0,1:T(8,128)S(1)} reduce(f32[8,16,864]{0,2,1:T(8,128)} %bitcast.30, f32[]{:T(128)} %constant.5.clone.1), dimensions={1}, to_apply=%region_3.0 | reduce | flops 103680 | bytes 470020 | tf_op jit(solution)/shard_map/reduce_sum | solution.py:34
  169.5 0.1 copy.21
  169.6 0.6 multiply_reduce_fusion
  171.0 0.6 fusion.14
  171.6 38.7 %all-gather = bf16[16,864,8]{1,2,0:T(8,128)(2,1)S(1)} all-gather(bf16[1,864,8]{1,2,0:T(8,128)(2,1)S(1)} %get-tuple-element.10), channel_id=1, replica_groups=mesh['node'=2,'dp'=16] {'dp'}, dimensions={0}, use_global_device_ids=true | all-gather | bytes 235008 | tf_op jit(solution)/shard_map/all_gather | solution.py:38
  210.4 0.2 reshape.50
  210.6 0.2 fusion.11
  210.8 2.1 all_gather.7
  212.9 0.8 copy.24
  (9 shorter events, 0.0 us)
Async XLA Ops:
  7.2 0.7 copy-start
  7.2 26.1 %copy-start.1 = (f32[1,8,13824]{2,1,0:T(8,128)S(1)}, f32[1,8,13824]{2,1,0:T(8,128)}, u32[]{:S(2)}) copy-start(f32[1,8,13824]{2,1,0:T(8,128)} %param.10) | copy-start | bytes 1327108
  7.2 26.1 %copy-start.2 = (f32[1,8,13824]{2,1,0:T(8,128)S(1)}, f32[1,8,13824]{2,1,0:T(8,128)}, u32[]{:S(2)}) copy-start(f32[1,8,13824]{2,1,0:T(8,128)} %param.9) | copy-start | bytes 1327108
  7.2 14.2 %reduce-scatter.3.cloned.1.call-start = ((), (), s32[]{:S(2)}) async-start(), calls=%async_computation.3 | async-start | bytes 663552 | tf_op jit(solution)/shard_map/reduce_scatter | solution.py:17
  10.5 22.8 %reduce-scatter.5.cloned.1.call-start = ((), (), s32[]{:S(2)}) async-start(), calls=%async_computation.4 | async-start | bytes 663552 | tf_op jit(solution)/shard_map/reduce_scatter | solution.py:17
  128.8 16.4 %all-to-all-start = ((bf16[16,2,3456]{2,1,0:T(2,128)(2,1)}), bf16[16,2,3456]{2,1,0:T(2,128)(2,1)S(1)}, u32[]{:S(2)}, u32[]{:S(2)}) async-start(bf16[16,2,3456]{2,1,0:T(2,128)(2,1)} %reshape.51), calls=%async_computation.2 | async-start | bytes 442368 | tf_op jit(solution)/shard_map/all_to_all | solution.py:33
  165.8 3.8 %copy-start.5 = (f32[8,864]{1,0:T(8,128)S(1)}, f32[8,864]{1,0:T(8,128)}, u32[]{:S(2)}) copy-start(f32[8,864]{1,0:T(8,128)} %param.11) | copy-start | bytes 82948
  165.8 44.7 %copy-start.3 = (f32[8,13824]{1,0:T(8,128)S(1)}, f32[8,13824]{1,0:T(8,128)}, u32[]{:S(2)}) copy-start(f32[8,13824]{1,0:T(8,128)} %param.12) | copy-start | bytes 1327108
  165.8 44.7 %copy-start.4 = (f32[8,13824]{1,0:T(8,128)S(1)}, f32[8,13824]{1,0:T(8,128)}, u32[]{:S(2)}) copy-start(f32[8,13824]{1,0:T(8,128)} %param.13) | copy-start | bytes 1327108
Sparse Core Ops, SparseCore 0:
  10.8 10.5 reduce-scatter.2
  24.3 8.9 reduce-scatter.4
where the time goes:
time: 221 us
  other arithmetic  95.7 us (43%)
  blocking collectives  40.9 us (19%)
  local copies, waits for them, and re-layouts  28.7 us (13%)
  waiting for transfers between devices  27.8 us (13%)
  between operations  15.5 us (7%)
  starting transfers between devices  6.83 us (3%)
  matrix products  5.19 us (2%)
    unnamed x2, other arithmetic  75.9 us
    all_gather x1, blocking collectives, body(): averaged = lax.all_gather(returned, 'dp', axis=1, tiled=True)  38.7 us
    reduce_scatter x2, waiting for transfers between devices, half_sum(): lax.psum_scatter(jnp.einsum('tc,tf->cf', local_cotan, acts_half, preferre...  20.1 us
    unnamed x16, local copies, waits for them, and re-layouts  17.6 us
    convert_element_type x1, local copies, waits for them, and re-layouts, body(): (worker_scale * jnp.tanh(carried / worker_scale)).astype(jnp.bfloat16)  10.7 us
    convert_element_type x1, other arithmetic, body(): arrived.astype(jnp.float32)  9.53 us
    all_to_all x1, waiting for transfers between devices, body(): lax.all_to_all(outgoing[None], 'dp', split_axis=2, concat_axis=0, tiled=T...  7.57 us
    all_to_all x1, starting transfers between devices, body(): lax.all_to_all(outgoing[None], 'dp', split_axis=2, concat_axis=0, tiled=T...  6.75 us
  transfers between devices with their start and end apart: 3, of which 3 were waited for; matrix products, arithmetic and copies ran while one was open for 2% of the time, Pallas kernels for 0%

commit v1 on v0

v1 whole, which is shorter than its diff:
```python
import functools

import jax
import jax.numpy as jnp
from jax import lax
from jax.experimental import pallas as pl
from jax.experimental.pallas import tpu as pltpu
from jax.sharding import PartitionSpec as P

beta_one = 0.9
epsilon = 1e-06
learn_rate = 0.5
LANES = 128

VMEM = pl.BlockSpec(memory_space=pltpu.VMEM)
ANY = pl.BlockSpec(memory_space=pl.ANY)


def chunk_count(cols, most):
    if cols % LANES:
        return 1
    return max(n for n in range(1, most + 1) if (cols // LANES) % n == 0)


def gradient_kernel(cotan_ref, acts_hbm, mine_ref, theirs_ref, acts, sems):
    rows = cotan_ref.shape[0]
    own = mine_ref.shape[0]
    chunks = sems.shape[0]
    width = acts.shape[1] // chunks
    spans = [pl.ds(i * width, width) for i in range(chunks)]
    copies = [pltpu.make_async_copy(acts_hbm.at[:, s], acts.at[:, s], sems.at[i]) for i, s in enumerate(spans)]
    for copy in copies:
        copy.start()
    shift = lax.rem(rows - lax.axis_index("node") * own, rows)
    cotan = pltpu.roll(cotan_ref[...].astype(jnp.float32), shift, 0).astype(jnp.bfloat16)
    for copy, s in zip(copies, spans):
        copy.wait()
        sums = jnp.dot(cotan, acts[:, s], preferred_element_type=jnp.float32)
        mine_ref[:, s] = sums[:own]
        for k in range(theirs_ref.shape[0]):
            theirs_ref[k, :, s] = sums[(k + 1) * own : (k + 2) * own]


def moment_of(momentum_ref, mine_ref, arrived_refs):
    gradient = mine_ref[...]
    for ref in arrived_refs:
        gradient = gradient + ref[...]
    return beta_one * momentum_ref[...] + (1.0 - beta_one) * gradient


def compress(values):
    scale = jnp.sqrt(jnp.mean(values * values, keepdims=True) + epsilon)
    return (scale * jnp.tanh(values / scale)).astype(jnp.bfloat16)


def send_kernel(momentum_ref, error_ref, mine_ref, *refs):
    arrived_refs, (blocks_ref, carried_ref, sent_ref) = refs[:-3], refs[-3:]
    carried = moment_of(momentum_ref, mine_ref, arrived_refs) + error_ref[...]
    carried_ref[...] = carried
    sent = compress(carried)
    sent_ref[...] = sent
    width = blocks_ref.shape[2]
    for i in range(blocks_ref.shape[0]):
        blocks_ref[i] = sent[:, i * width : (i + 1) * width]


def keep_kernel(momentum_ref, carried_ref, sent_ref, master_hbm, second_hbm, mine_ref, *refs):
    arrived_refs = refs[:-7]
    moment_ref, error_ref, master_ref, bottom_ref, window, sem_a, sem_b = refs[-7:]
    width, span, cols = master_ref.shape[1], window.shape[2], master_hbm.shape[1]
    column = lax.axis_index("dp") * width
    start = jnp.minimum((column // LANES) * LANES, cols - span)
    here = pl.ds(pl.multiple_of(start, LANES), span)
    copy_a = pltpu.make_async_copy(master_hbm.at[:, here], window.at[0], sem_a)
    copy_b = pltpu.make_async_copy(second_hbm.at[:, here], window.at[1], sem_b)
    copy_a.start()
    copy_b.start()
    moment_ref[...] = moment_of(momentum_ref, mine_ref, arrived_refs)
    error_ref[...] = carried_ref[...] - sent_ref[...].astype(jnp.float32)
    shift = lax.rem(span - (column - start), span)
    copy_a.wait()
    copy_b.wait()
    master_ref[...] = pltpu.roll(window[0], shift, 1)[:, :width]
    bottom_ref[...] = jnp.sqrt(pltpu.roll(window[1], shift, 1)[:, :width]) + 1e-08


def serve_kernel(blocks_ref, error_ref, master_ref, bottom_ref, new_error_ref, out_ref):
    replicas = blocks_ref.shape[0]
    total = blocks_ref[0].astype(jnp.float32)
    for i in range(1, replicas):
        total = total + blocks_ref[i].astype(jnp.float32)
    served = total / replicas + error_ref[...]
    returned = compress(served).astype(jnp.float32)
    new_error_ref[...] = served - returned
    weights = (master_ref[...] - learn_rate * (returned / bottom_ref[...])).astype(jnp.bfloat16)
    for i in range(replicas):
        out_ref[i] = weights


def assemble_kernel(*refs):
    parts, out_ref = refs[:-1], refs[-1]
    nodes = len(parts)
    servers, own, width = parts[0].shape
    me = lax.axis_index("node")
    for i in range(servers):
        loaded = [part[i].astype(jnp.float32) for part in parts]
        stacked = []
        for node in range(nodes):
            chosen = loaded[0]
            for k in range(1, nodes):
                chosen = jnp.where(lax.rem(me - k + nodes, nodes) == node, loaded[k], chosen)
            stacked.append(chosen)
        out_ref[:, i * width : (i + 1) * width] = jnp.concatenate(stacked, axis=0).astype(jnp.bfloat16)


def body(hidden, cotangent, momentum, worker_error, server_error, master, second_moment):
    f32, bf16 = jnp.float32, jnp.bfloat16
    nodes, servers = lax.axis_size("node"), lax.axis_size("dp")
    tokens, cols = hidden.shape[1:]
    rows, own = cotangent.shape[2], momentum.shape[1]
    width = cols // servers
    shape = jax.ShapeDtypeStruct

    def turn(value, k):
        return lax.ppermute(value, "node", [(i, (i + k) % nodes) for i in range(nodes)])

    chunks = chunk_count(cols, 6)
    mine, theirs = pl.pallas_call(
        gradient_kernel,
        name="gradient",
        out_shape=(shape((own, cols), f32), shape((nodes - 1, own, cols), f32)),
        in_specs=[VMEM, ANY],
        out_specs=(VMEM, VMEM),
        scratch_shapes=[pltpu.VMEM((tokens, cols), bf16), pltpu.SemaphoreType.DMA((chunks,))],
    )(cotangent[0].T, hidden[0])
    arrived = [turn(theirs[k - 1], k) for k in range(1, nodes)]

    blocks, carried, sent = pl.pallas_call(
        send_kernel,
        name="send",
        out_shape=(shape((servers, own, width), bf16), shape((own, cols), f32), shape((own, cols), bf16)),
        in_specs=[VMEM] * (3 + len(arrived)),
        out_specs=(VMEM, VMEM, VMEM),
    )(momentum[0], worker_error[0], mine, *arrived)
    gathered = lax.all_to_all(blocks, "dp", split_axis=0, concat_axis=0, tiled=True)

    span = min(cols, -(-width // LANES) * LANES + LANES)
    moment, new_worker, master_part, bottom = pl.pallas_call(
        keep_kernel,
        name="keep",
        out_shape=(shape((own, cols), f32), shape((own, cols), f32), shape((own, width), f32), shape((own, width), f32)),
        in_specs=[VMEM, VMEM, VMEM, ANY, ANY] + [VMEM] * (1 + len(arrived)),
        out_specs=(VMEM, VMEM, VMEM, VMEM),
        scratch_shapes=[pltpu.VMEM((2, own, span), f32), pltpu.SemaphoreType.DMA(()), pltpu.SemaphoreType.DMA(())],
    )(momentum[0], carried, sent, master, second_moment, mine, *arrived)

    new_server, copies = pl.pallas_call(
        serve_kernel,
        name="serve",
        out_shape=(shape((own, width), f32), shape((servers, own, width), bf16)),
        in_specs=[VMEM] * 4,
        out_specs=(VMEM, VMEM),
    )(gathered, server_error, master_part, bottom)
    everyone = lax.all_to_all(copies, "dp", split_axis=0, concat_axis=0, tiled=True)
    parts = [everyone] + [turn(everyone, k) for k in range(1, nodes)]

    weights = pl.pallas_call(
        assemble_kernel,
        name="assemble",
        out_shape=shape((rows, cols), bf16),
        in_specs=[VMEM] * nodes,
        out_specs=VMEM,
    )(*parts)
    return (moment[None], new_worker[None], new_server, weights)


def solution(mesh):
    placed = (
        P("dp", "node", None),
        P("dp", "node", None),
        P("dp", "node", None),
        P("dp", "node", None),
        P("node", "dp"),
        P("node", None),
        P("node", None),
    )
    return jax.shard_map(
        body,
        mesh=mesh,
        in_specs=placed,
        out_specs=(P("dp", "node", None), P("dp", "node", None), P("node", "dp"), P()),
        check_vma=False,
    )
```

time: 221 us -> 47.4 us (0.21)
  other arithmetic: 95.7 us -> 0 us
  blocking collectives: 40.9 us -> 12.2 us
  local copies, waits for them, and re-layouts: 28.7 us -> 2.14 us
  waiting for transfers between devices: 27.8 us -> 9.46 us
  between operations: 15.5 us -> 0.66 us
  Pallas kernels: 0 us -> 13.6 us
  matrix products: 5.19 us -> 0 us
    unnamed x2 -> x0, other arithmetic: 75.9 us -> none
    all_gather x2 -> x0, blocking collectives: 40.9 us -> none  [the longest x1 38.7 us: body(): averaged = lax.all_gather(returned, 'dp', axis=1, tiled=True)]
    reduce_scatter x2 -> x0, waiting for transfers between devices: 20.1 us -> none  [half_sum(): lax.psum_scatter(jnp.einsum('tc,tf->cf', local_cotan, acts_half, preferre...]
    unnamed x16 -> x8, local copies, waits for them, and re-layouts: 17.6 us -> 2.14 us
    pallas_call x0 -> x5, Pallas kernels: none -> 13.6 us  [the longest x1 3.92 us: body(): pl.pallas_call(gradient_kernel, name='gradient', out_shape=(shape((own, c...]
    all_to_all x0 -> x1, blocking collectives: none -> 12.2 us  [body(): lax.all_to_all(copies, 'dp', split_axis=0, concat_axis=0, tiled=True)]
    convert_element_type x3 -> x0, other arithmetic: 11.7 us -> none  [the longest x1 9.53 us: body(): arrived.astype(jnp.float32)]
    convert_element_type x3 -> x0, local copies, waits for them, and re-layouts: 10.9 us -> none  [the longest x1 10.7 us: body(): (worker_scale * jnp.tanh(carried / worker_scale)).astype(jnp.bfloat16)]
  transfers between devices with their start and end apart: 3 -> 3, of which waited for: 3 -> 3; matrix products, arithmetic and copies ran while one was open for 2% -> 0% of each run, Pallas kernels for 0% -> 7%
where the time goes in v1:
time: 47.4 us; the launch traced here: 46.9 us
  Pallas kernels  13.6 us (29%)
  blocking collectives  12.2 us (26%)
  waiting for transfers between devices  9.46 us (20%)
  starting transfers between devices  8.78 us (19%)
  local copies, waits for them, and re-layouts  2.14 us (5%)
  between operations  0.66 us (1%)
    all_to_all x1, blocking collectives, body(): lax.all_to_all(copies, 'dp', split_axis=0, concat_axis=0, tiled=True)  12.2 us
    all_to_all x1, starting transfers between devices, body(): lax.all_to_all(blocks, 'dp', split_axis=0, concat_axis=0, tiled=True)  8.22 us
    all_to_all x1, waiting for transfers between devices, body(): lax.all_to_all(blocks, 'dp', split_axis=0, concat_axis=0, tiled=True)  6.34 us
    pallas_call x1, Pallas kernels, body(): pl.pallas_call(gradient_kernel, name='gradient', out_shape=(shape((own, c...  3.92 us
    pallas_call x1, Pallas kernels, body(): pl.pallas_call(keep_kernel, name='keep', out_shape=(shape((own, cols), f3...  3.21 us
    ppermute x2, waiting for transfers between devices, turn(): lax.ppermute(value, 'node', [(i, (i + k) % nodes) for i in range(nodes)])  3.12 us
    pallas_call x1, Pallas kernels, body(): pl.pallas_call(send_kernel, name='send', out_shape=(shape((servers, own,...  2.67 us
    unnamed x8, local copies, waits for them, and re-layouts  2.14 us
  transfers between devices with their start and end apart: 3, of which 3 were waited for; matrix products, arithmetic and copies ran while one was open for 0% of the time, Pallas kernels for 7%

profile of v1, /device:TPU:0, one launch (start us, length us, event | category | flops | bytes accessed | tf_op | source)
XLA Modules:
  0.0 46.9 jit_solution(781183264563093991)
XLA Ops:
  0.6 3.9 %gradient.1 = (f32[8,13824]{1,0:T(8,128)}, f32[1,8,13824]{2,1,0:T(8,128)}) custom-call(bf16[16,128]{1,0:T(8,128)(2,1)} %bitcast.13, bf16[128,13824]{1,0:T(8,128)(2,1)} %bitcast.9), custom_call_target="tpu_custom_call" | custom-call | tf_op jit(solution)/shard_map/gradient/pallas_call | solution.py:128
  4.6 0.6 %collective-permute-start = (f32[8,13824]{1,0:T(8,128)}, f32[8,13824]{1,0:T(8,128)S(1)}, u32[]{:S(2)}, u32[]{:S(2)}) collective-permute-start(f32[8,13824]{1,0:T(8,128)} %bitcast.16), channel_id=1, source_target_pairs={{0,16},{16,0},{1,17},{17,1},{2,18},{18,2},{3,19},{19,3},{4,20},{20... | collective-permute-start | bytes 1327112 | tf_op jit(solution)/shard_map/ppermute | solution.py:125
  5.1 1.6 %collective-permute-done.refs_0_ = f32[8,13824]{1,0:T(8,128)S(1)} collective-permute-done((f32[8,13824]{1,0:T(8,128)}, f32[8,13824]{1,0:T(8,128)S(1)}, u32[]{:S(2)}, u32[]{:S(2)}) %collective-permute-start) | collective-permute-done | bytes 442400 | tf_op jit(solution)/shard_map/ppermute | solution.py:125
  6.7 0.0 copy-start
  6.7 0.8 %copy-done = f32[8,13824]{1,0:T(8,128)} copy-done((f32[8,13824]{1,0:T(8,128)}, f32[8,13824]{1,0:T(8,128)S(1)}, u32[]{:S(2)}) %copy-start) | copy-done | bytes 442392
  7.5 2.7 %send.1 = (bf16[16,8,864]{2,1,0:T(8,128)(2,1)}, f32[8,13824]{1,0:T(8,128)}, bf16[8,13824]{1,0:T(8,128)(2,1)}) custom-call(f32[8,13824]{1,0:T(8,128)} %bitcast.10, f32[8,13824]{1,0:T(8,128)} %bitcast.12, f32[8,13824]{1,0:T(8,128)} %get-tuple-element.15.mine_ref, f32[8,13824]{1,0:T(8,128)} %copy-done), custom_call_target="tpu_custom_call" | custom-call | tf_op jit(solution)/shard_map/send/pallas_call | solution.py:138
  10.2 8.2 %all-to-all-start = ((bf16[16,8,864]{2,1,0:T(8,128)(2,1)}), bf16[16,8,864]{2,1,0:T(8,128)(2,1)S(1)}, u32[]{:S(2)}, u32[]{:S(2)}) async-start(bf16[16,8,864]{2,1,0:T(8,128)(2,1)} %get-tuple-element.21), calls=%async_computation | async-start | bytes 458752 | tf_op jit(solution)/shard_map/all_to_all | solution.py:145
  18.4 3.2 %keep.1 = (f32[8,13824]{1,0:T(8,128)}, f32[8,13824]{1,0:T(8,128)}, f32[8,864]{1,0:T(8,128)}, f32[8,864]{1,0:T(8,128)}) custom-call(f32[8,13824]{1,0:T(8,128)} %bitcast.11, f32[8,13824]{1,0:T(8,128)} %get-tuple-element.17.carried_ref, bf16[8,13824]{1,0:T(8,128)(2,1)} %get-tuple-element.18.sent_ref, f32[8,13824]{1,0:T(8,128)} %master_hbm.1, ...), custom_call_target="tpu_custom_call" | custom-call | tf_op jit(solution)/shard_map/keep/pallas_call | solution.py:148
  21.6 6.3 %all-to-all-done.blocks_ref = bf16[16,8,864]{2,1,0:T(8,128)(2,1)S(1)} async-done(((bf16[16,8,864]{2,1,0:T(8,128)(2,1)}), bf16[16,8,864]{2,1,0:T(8,128)(2,1)S(1)}, u32[]{:S(2)}, u32[]{:S(2)}) %all-to-all-start) | async-done | bytes 221216 | tf_op jit(solution)/shard_map/all_to_all | solution.py:145
  28.0 0.0 copy-start.2
  28.0 0.7 %copy-done.2 = bf16[16,8,864]{2,1,0:T(8,128)(2,1)} copy-done((bf16[16,8,864]{2,1,0:T(8,128)(2,1)}, bf16[16,8,864]{2,1,0:T(8,128)(2,1)S(1)}, u32[]{:S(2)}) %copy-start.2) | copy-done | bytes 221208
  28.7 1.8 %serve.1 = (f32[8,864]{1,0:T(8,128)}, bf16[16,8,864]{2,1,0:T(8,128)(2,1)}) custom-call(bf16[16,8,864]{2,1,0:T(8,128)(2,1)} %copy-done.2, f32[8,864]{1,0:T(8,128)} %error_ref.1, f32[8,864]{1,0:T(8,128)} %get-tuple-element.22.master_ref, f32[8,864]{1,0:T(8,128)} %get-tuple-element.23.bottom_ref), custom_call_target="tpu_custom_call" | custom-call | tf_op jit(solution)/shard_map/serve/pallas_call | solution.py:157
  30.5 12.2 %all_to_all.10.refs_0_ = bf16[16,8,864]{2,1,0:T(8,128)(2,1)S(1)} all-to-all(bf16[16,8,864]{2,1,0:T(8,128)(2,1)} %get-tuple-element.25), channel_id=1, replica_groups=mesh['node'=2,'dp'=16] {'dp'}, dimensions={0} | all-to-all | bytes 442368 | tf_op jit(solution)/shard_map/all_to_all | solution.py:164
  42.7 0.0 copy-start.1
  42.7 0.0 collective-permute-start.1
  42.7 1.5 %collective-permute-done.1.refs_1_ = bf16[16,8,864]{2,1,0:T(8,128)(2,1)S(1)} collective-permute-done((bf16[16,8,864]{2,1,0:T(8,128)(2,1)S(1)}, bf16[16,8,864]{2,1,0:T(8,128)(2,1)S(1)}, u32[]{:S(2)}, u32[]{:S(2)}) %collective-permute-start.1) | collective-permute-done | bytes 221216 | tf_op jit(solution)/shard_map/ppermute | solution.py:125
  44.2 0.0 copy-done.1
  44.2 0.0 copy-start.3
  44.2 0.7 %copy-done.3 = bf16[16,8,864]{2,1,0:T(8,128)(2,1)} copy-done((bf16[16,8,864]{2,1,0:T(8,128)(2,1)}, bf16[16,8,864]{2,1,0:T(8,128)(2,1)S(1)}, u32[]{:S(2)}) %copy-start.3) | copy-done | bytes 221208
  44.9 2.0 %assemble.1 = bf16[16,13824]{1,0:T(8,128)(2,1)} custom-call(bf16[16,8,864]{2,1,0:T(8,128)(2,1)} %copy-done.1, bf16[16,8,864]{2,1,0:T(8,128)(2,1)} %copy-done.3), custom_call_target="tpu_custom_call" | custom-call | tf_op jit(solution)/shard_map/assemble/pallas_call | solution.py:167
Async XLA Ops:
  4.6 2.2 %collective-permute-start = (f32[8,13824]{1,0:T(8,128)}, f32[8,13824]{1,0:T(8,128)S(1)}, u32[]{:S(2)}, u32[]{:S(2)}) collective-permute-start(f32[8,13824]{1,0:T(8,128)} %bitcast.16), channel_id=1, source_target_pairs={{0,16},{16,0},{1,17},{17,1},{2,18},{18,2},{3,19},{19,3},{4,20},{20... | collective-permute-start | bytes 1327112 | tf_op jit(solution)/shard_map/ppermute | solution.py:125
  6.7 0.8 %copy-start = (f32[8,13824]{1,0:T(8,128)}, f32[8,13824]{1,0:T(8,128)S(1)}, u32[]{:S(2)}) copy-start(f32[8,13824]{1,0:T(8,128)S(1)} %collective-permute-done.refs_0_) | copy-start | bytes 1327108
  10.2 17.8 %all-to-all-start = ((bf16[16,8,864]{2,1,0:T(8,128)(2,1)}), bf16[16,8,864]{2,1,0:T(8,128)(2,1)S(1)}, u32[]{:S(2)}, u32[]{:S(2)}) async-start(bf16[16,8,864]{2,1,0:T(8,128)(2,1)} %get-tuple-element.21), calls=%async_computation | async-start | bytes 458752 | tf_op jit(solution)/shard_map/all_to_all | solution.py:145
  28.0 0.7 %copy-start.2 = (bf16[16,8,864]{2,1,0:T(8,128)(2,1)}, bf16[16,8,864]{2,1,0:T(8,128)(2,1)S(1)}, u32[]{:S(2)}) copy-start(bf16[16,8,864]{2,1,0:T(8,128)(2,1)S(1)} %all-to-all-done.blocks_ref) | copy-start | bytes 663556
  42.7 1.5 %copy-start.1 = (bf16[16,8,864]{2,1,0:T(8,128)(2,1)}, bf16[16,8,864]{2,1,0:T(8,128)(2,1)S(1)}, u32[]{:S(2)}) copy-start(bf16[16,8,864]{2,1,0:T(8,128)(2,1)S(1)} %all_to_all.10.refs_0_) | copy-start | bytes 663556
  42.7 1.5 %collective-permute-start.1 = (bf16[16,8,864]{2,1,0:T(8,128)(2,1)S(1)}, bf16[16,8,864]{2,1,0:T(8,128)(2,1)S(1)}, u32[]{:S(2)}, u32[]{:S(2)}) collective-permute-start(bf16[16,8,864]{2,1,0:T(8,128)(2,1)S(1)} %all_to_all.10.refs_0_), channel_id=1, source_target_pairs={{0,16},{16,0},{1,17},{17,1},{2,18},{18,2},{3,19},{19,3},{4,20},{20... | collective-permute-start | bytes 663560 | tf_op jit(solution)/shard_map/ppermute | solution.py:125
  44.2 0.7 %copy-start.3 = (bf16[16,8,864]{2,1,0:T(8,128)(2,1)}, bf16[16,8,864]{2,1,0:T(8,128)(2,1)S(1)}, u32[]{:S(2)}) copy-start(bf16[16,8,864]{2,1,0:T(8,128)(2,1)S(1)} %collective-permute-done.1.refs_1_) | copy-start | bytes 663556

commit v2 on v1

--- a/solution.py
+++ b/solution.py
@@ -13,7 +13,16 @@
 LANES = 128
 
 VMEM = pl.BlockSpec(memory_space=pltpu.VMEM)
-ANY = pl.BlockSpec(memory_space=pl.ANY)
+HBM = pl.BlockSpec(memory_space=pltpu.HBM)
+MIB = 2**20
+
+
+def near(*values):
+    return [pltpu.with_memory_space_constraint(v, pltpu.VMEM) for v in values]
+
+
+def far(*values):
+    return [pltpu.with_memory_space_constraint(v, pltpu.HBM) for v in values]
 
 
 def chunk_count(cols, most):
@@ -22,30 +31,38 @@
     return max(n for n in range(1, most + 1) if (cols // LANES) % n == 0)
 
 
-def gradient_kernel(cotan_ref, acts_hbm, mine_ref, theirs_ref, acts, sems):
+def gradient_kernel(cotan_hbm, momentum_hbm, acts_hbm, base_ref, theirs_ref, cotan_ref, acts, sems, cotan_sem, base_sem):
     rows = cotan_ref.shape[0]
-    own = mine_ref.shape[0]
+    own = base_ref.shape[0]
     chunks = sems.shape[0]
     width = acts.shape[1] // chunks
     spans = [pl.ds(i * width, width) for i in range(chunks)]
+    cotan_copy = pltpu.make_async_copy(cotan_hbm, cotan_ref, cotan_sem)
+    base_copy = pltpu.make_async_copy(momentum_hbm, base_ref, base_sem)
     copies = [pltpu.make_async_copy(acts_hbm.at[:, s], acts.at[:, s], sems.at[i]) for i, s in enumerate(spans)]
-    for copy in copies:
+    cotan_copy.start()
+    copies[0].start()
+    base_copy.start()
+    for copy in copies[1:]:
         copy.start()
     shift = lax.rem(rows - lax.axis_index("node") * own, rows)
+    cotan_copy.wait()
     cotan = pltpu.roll(cotan_ref[...].astype(jnp.float32), shift, 0).astype(jnp.bfloat16)
-    for copy, s in zip(copies, spans):
+    for i, (copy, s) in enumerate(zip(copies, spans)):
         copy.wait()
+        if i == 0:
+            base_copy.wait()
         sums = jnp.dot(cotan, acts[:, s], preferred_element_type=jnp.float32)
-        mine_ref[:, s] = sums[:own]
+        base_ref[:, s] = beta_one * base_ref[:, s] + (1.0 - beta_one) * sums[:own]
         for k in range(theirs_ref.shape[0]):
             theirs_ref[k, :, s] = sums[(k + 1) * own : (k + 2) * own]
 
 
-def moment_of(momentum_ref, mine_ref, arrived_refs):
-    gradient = mine_ref[...]
-    for ref in arrived_refs:
-        gradient = gradient + ref[...]
-    return beta_one * momentum_ref[...] + (1.0 - beta_one) * gradient
+def moment_of(base_ref, arrived_refs):
+    rest = arrived_refs[0][...]
+    for ref in arrived_refs[1:]:
+        rest = rest + ref[...]
+    return base_ref[...] + (1.0 - beta_one) * rest
 
 
 def compress(values):
@@ -53,9 +70,9 @@
     return (scale * jnp.tanh(values / scale)).astype(jnp.bfloat16)
 
 
-def send_kernel(momentum_ref, error_ref, mine_ref, *refs):
+def send_kernel(error_ref, base_ref, *refs):
     arrived_refs, (blocks_ref, carried_ref, sent_ref) = refs[:-3], refs[-3:]
-    carried = moment_of(momentum_ref, mine_ref, arrived_refs) + error_ref[...]
+    carried = moment_of(base_ref, arrived_refs) + error_ref[...]
     carried_ref[...] = carried
     sent = compress(carried)
     sent_ref[...] = sent
@@ -64,7 +81,7 @@
         blocks_ref[i] = sent[:, i * width : (i + 1) * width]
 
 
-def keep_kernel(momentum_ref, carried_ref, sent_ref, master_hbm, second_hbm, mine_ref, *refs):
+def keep_kernel(carried_ref, sent_ref, master_hbm, second_hbm, base_ref, *refs):
     arrived_refs = refs[:-7]
     moment_ref, error_ref, master_ref, bottom_ref, window, sem_a, sem_b = refs[-7:]
     width, span, cols = master_ref.shape[1], window.shape[2], master_hbm.shape[1]
@@ -75,7 +92,7 @@
     copy_b = pltpu.make_async_copy(second_hbm.at[:, here], window.at[1], sem_b)
     copy_a.start()
     copy_b.start()
-    moment_ref[...] = moment_of(momentum_ref, mine_ref, arrived_refs)
+    moment_ref[...] = moment_of(base_ref, arrived_refs)
     error_ref[...] = carried_ref[...] - sent_ref[...].astype(jnp.float32)
     shift = lax.rem(span - (column - start), span)
     copy_a.wait()
@@ -124,53 +141,55 @@
     def turn(value, k):
         return lax.ppermute(value, "node", [(i, (i + k) % nodes) for i in range(nodes)])
 
+    def call(kernel, name, outs, specs, scratch=(), limit=16 * MIB):
+        return pl.pallas_call(
+            kernel,
+            name=name,
+            out_shape=outs,
+            in_specs=specs,
+            out_specs=jax.tree.map(lambda _: VMEM, outs),
+            scratch_shapes=scratch,
+            compiler_params=pltpu.CompilerParams(vmem_limit_bytes=limit),
+        )
+
     chunks = chunk_count(cols, 6)
-    mine, theirs = pl.pallas_call(
+    base, theirs = call(
         gradient_kernel,
-        name="gradient",
-        out_shape=(shape((own, cols), f32), shape((nodes - 1, own, cols), f32)),
-        in_specs=[VMEM, ANY],
-        out_specs=(VMEM, VMEM),
-        scratch_shapes=[pltpu.VMEM((tokens, cols), bf16), pltpu.SemaphoreType.DMA((chunks,))],
-    )(cotangent[0].T, hidden[0])
+        "gradient",
+        (pltpu.VMEM((own, cols), f32), pltpu.VMEM((nodes - 1, own, cols), f32)),
+        [HBM] * 3,
+        [pltpu.VMEM((rows, tokens), bf16), pltpu.VMEM((tokens, cols), bf16), pltpu.SemaphoreType.DMA((chunks,))]
+        + [pltpu.SemaphoreType.DMA(())] * 2,
+    )(*far(cotangent[0].T, momentum[0], hidden[0]))
     arrived = [turn(theirs[k - 1], k) for k in range(1, nodes)]
 
-    blocks, carried, sent = pl.pallas_call(
+    blocks, carried, sent = call(
         send_kernel,
-        name="send",
-        out_shape=(shape((servers, own, width), bf16), shape((own, cols), f32), shape((own, cols), bf16)),
-        in_specs=[VMEM] * (3 + len(arrived)),
-        out_specs=(VMEM, VMEM, VMEM),
-    )(momentum[0], worker_error[0], mine, *arrived)
+        "send",
+        (pltpu.VMEM((servers, own, width), bf16), pltpu.VMEM((own, cols), f32), pltpu.VMEM((own, cols), bf16)),
+        [VMEM] * (2 + len(arrived)),
+    )(*near(worker_error[0], base, *arrived))
     gathered = lax.all_to_all(blocks, "dp", split_axis=0, concat_axis=0, tiled=True)
 
     span = min(cols, -(-width // LANES) * LANES + LANES)
-    moment, new_worker, master_part, bottom = pl.pallas_call(
+    moment, new_worker, master_part, bottom = call(
         keep_kernel,
-        name="keep",
-        out_shape=(shape((own, cols), f32), shape((own, cols), f32), shape((own, width), f32), shape((own, width), f32)),
-        in_specs=[VMEM, VMEM, VMEM, ANY, ANY] + [VMEM] * (1 + len(arrived)),
-        out_specs=(VMEM, VMEM, VMEM, VMEM),
-        scratch_shapes=[pltpu.VMEM((2, own, span), f32), pltpu.SemaphoreType.DMA(()), pltpu.SemaphoreType.DMA(())],
-    )(momentum[0], carried, sent, master, second_moment, mine, *arrived)
-
-    new_server, copies = pl.pallas_call(
+        "keep",
+        (shape((own, cols), f32), shape((own, cols), f32), pltpu.VMEM((own, width), f32), pltpu.VMEM((own, width), f32)),
+        [VMEM, VMEM, HBM, HBM] + [VMEM] * (1 + len(arrived)),
+        [pltpu.VMEM((2, own, span), f32), pltpu.SemaphoreType.DMA(()), pltpu.SemaphoreType.DMA(())],
+    )(*near(carried, sent), *far(master, second_moment), *near(base, *arrived))
+
+    new_server, copies = call(
         serve_kernel,
-        name="serve",
-        out_shape=(shape((own, width), f32), shape((servers, own, width), bf16)),
-        in_specs=[VMEM] * 4,
-        out_specs=(VMEM, VMEM),
-    )(gathered, server_error, master_part, bottom)
+        "serve",
+        (shape((own, width), f32), pltpu.VMEM((servers, own, width), bf16)),
+        [VMEM] * 4,
+    )(*near(gathered, server_error, master_part, bottom))
     everyone = lax.all_to_all(copies, "dp", split_axis=0, concat_axis=0, tiled=True)
     parts = [everyone] + [turn(everyone, k) for k in range(1, nodes)]
 
-    weights = pl.pallas_call(
-        assemble_kernel,
-        name="assemble",
-        out_shape=shape((rows, cols), bf16),
-        in_specs=[VMEM] * nodes,
-        out_specs=VMEM,
-    )(*parts)
+    weights = call(assemble_kernel, "assemble", shape((rows, cols), bf16), [VMEM] * nodes)(*near(*parts))
     return (moment[None], new_worker[None], new_server, weights)
 
 

time: 47.4 us -> 40.4 us (0.85)
  Pallas kernels: 13.6 us -> 7.87 us
  local copies, waits for them, and re-layouts: 2.14 us -> 0.01 us
  waiting for transfers between devices: 9.46 us -> 10.7 us
    pallas_call x5, Pallas kernels: 13.6 us -> 7.87 us  [the longest x1 3.25 us: body(): call(gradient_kernel, 'gradient', (pltpu.VMEM((own, cols), f32), pltpu.VM...]
    unnamed x8 -> x4, local copies, waits for them, and re-layouts: 2.14 us -> 0.01 us
    all_to_all x1, waiting for transfers between devices: 6.34 us -> 7.82 us  [body(): lax.all_to_all(blocks, 'dp', split_axis=0, concat_axis=0, tiled=True)]
  transfers between devices with their start and end apart: 3 -> 3, of which waited for: 3 -> 3; matrix products, arithmetic and copies ran while one was open for 0% -> 0% of each run, Pallas kernels for 7% -> 4%
where the time goes in v2:
time: 40.4 us; the launch traced here: 40.1 us
  blocking collectives  12 us (30%)
  waiting for transfers between devices  10.7 us (26%)
  starting transfers between devices  8.78 us (22%)
  Pallas kernels  7.87 us (19%)
  between operations  0.68 us (2%)
    all_to_all x1, blocking collectives, body(): lax.all_to_all(copies, 'dp', split_axis=0, concat_axis=0, tiled=True)  12 us
    all_to_all x1, starting transfers between devices, body(): lax.all_to_all(blocks, 'dp', split_axis=0, concat_axis=0, tiled=True)  8.22 us
    all_to_all x1, waiting for transfers between devices, body(): lax.all_to_all(blocks, 'dp', split_axis=0, concat_axis=0, tiled=True)  7.82 us
    pallas_call x1, Pallas kernels, body(): call(gradient_kernel, 'gradient', (pltpu.VMEM((own, cols), f32), pltpu.VM...  3.25 us
    ppermute x2, waiting for transfers between devices, turn(): lax.ppermute(value, 'node', [(i, (i + k) % nodes) for i in range(nodes)])  2.91 us
    pallas_call x1, Pallas kernels, body(): call(keep_kernel, 'keep', (shape((own, cols), f32), shape((own, cols), f3...  1.72 us
    pallas_call x1, Pallas kernels, body(): call(send_kernel, 'send', (pltpu.VMEM((servers, own, width), bf16), pltpu...  1.17 us
    pallas_call x1, Pallas kernels, body(): call(assemble_kernel, 'assemble', shape((rows, cols), bf16), [VMEM] * nodes)  0.94 us
  transfers between devices with their start and end apart: 3, of which 3 were waited for; matrix products, arithmetic and copies ran while one was open for 0% of the time, Pallas kernels for 4%

profile of v2, /device:TPU:0, one launch (start us, length us, event | category | flops | bytes accessed | tf_op | source)
XLA Modules:
  0.0 40.1 jit_solution(17625734444887409534)
XLA Ops:
  0.6 0.0 copy-start
  0.6 0.0 copy-start.1
  0.7 3.2 %gradient.1 = (f32[8,13824]{1,0:T(8,128)S(1)}, f32[1,8,13824]{2,1,0:T(8,128)S(1)}) custom-call(bf16[16,128]{1,0:T(8,128)(2,1)} %bitcast.13, f32[8,13824]{1,0:T(8,128)} %bitcast.12, bf16[128,13824]{1,0:T(8,128)(2,1)} %bitcast.11), custom_call_target="tpu_custom_call" | custom-call | tf_op jit(solution)/shard_map/gradient/pallas_call | solution.py:156
  3.9 0.6 %collective-permute-start = (f32[8,13824]{1,0:T(8,128)S(1)}, f32[8,13824]{1,0:T(8,128)S(1)}, u32[]{:S(2)}, u32[]{:S(2)}) collective-permute-start(f32[8,13824]{1,0:T(8,128)S(1)} %bitcast.10), channel_id=1, source_target_pairs={{0,16},{16,0},{1,17},{17,1},{2,18},{18,2},{3,19},{19,3},{4,20},{20... | collective-permute-start | bytes 1327112 | tf_op jit(solution)/shard_map/ppermute | solution.py:142
  4.5 1.4 %collective-permute-done.refs_0_ = f32[8,13824]{1,0:T(8,128)S(1)} collective-permute-done((f32[8,13824]{1,0:T(8,128)S(1)}, f32[8,13824]{1,0:T(8,128)S(1)}, u32[]{:S(2)}, u32[]{:S(2)}) %collective-permute-start) | collective-permute-done | bytes 442400 | tf_op jit(solution)/shard_map/ppermute | solution.py:142
  5.9 0.0 copy-done
  5.9 1.2 %send.1 = (bf16[16,8,864]{2,1,0:T(8,128)(2,1)}, f32[8,13824]{1,0:T(8,128)S(1)}, bf16[8,13824]{1,0:T(8,128)(2,1)S(1)}) custom-call(f32[8,13824]{1,0:T(8,128)S(1)} %bitcast.9, f32[8,13824]{1,0:T(8,128)S(1)} %get-tuple-element.15.base_ref, f32[8,13824]{1,0:T(8,128)S(1)} %collective-permute-done.refs_0_), custom_call_target="tpu_custom_call" | custom-call | tf_op jit(solution)/shard_map/send/pallas_call | solution.py:166
  7.1 8.2 %all-to-all-start = ((bf16[16,8,864]{2,1,0:T(8,128)(2,1)}), bf16[16,8,864]{2,1,0:T(8,128)(2,1)S(1)}, u32[]{:S(2)}, u32[]{:S(2)}) async-start(bf16[16,8,864]{2,1,0:T(8,128)(2,1)} %get-tuple-element.21), calls=%async_computation | async-start | bytes 458752 | tf_op jit(solution)/shard_map/all_to_all | solution.py:172
  15.3 1.7 %keep.1 = (f32[8,13824]{1,0:T(8,128)}, f32[8,13824]{1,0:T(8,128)}, f32[8,864]{1,0:T(8,128)S(1)}, f32[8,864]{1,0:T(8,128)S(1)}) custom-call(f32[8,13824]{1,0:T(8,128)S(1)} %get-tuple-element.17.carried_ref, bf16[8,13824]{1,0:T(8,128)(2,1)S(1)} %get-tuple-element.18.sent_ref, f32[8,13824]{1,0:T(8,128)} %master_hbm.1, f32[8,13824]{1,0:T(8,128)} %second_hbm.1, ...), custom_call_target="tpu_custom_call" | custom-call | tf_op jit(solution)/shard_map/keep/pallas_call | solution.py:175
  17.0 7.8 %all-to-all-done.blocks_ref = bf16[16,8,864]{2,1,0:T(8,128)(2,1)S(1)} async-done(((bf16[16,8,864]{2,1,0:T(8,128)(2,1)}), bf16[16,8,864]{2,1,0:T(8,128)(2,1)S(1)}, u32[]{:S(2)}, u32[]{:S(2)}) %all-to-all-start) | async-done | bytes 221216 | tf_op jit(solution)/shard_map/all_to_all | solution.py:172
  24.8 0.0 copy-done.1
  24.9 0.8 %serve.1 = (f32[8,864]{1,0:T(8,128)}, bf16[16,8,864]{2,1,0:T(8,128)(2,1)S(1)}) custom-call(bf16[16,8,864]{2,1,0:T(8,128)(2,1)S(1)} %all-to-all-done.blocks_ref, f32[8,864]{1,0:T(8,128)S(1)} %copy-done.1, f32[8,864]{1,0:T(8,128)S(1)} %get-tuple-element.22.master_ref, f32[8,864]{1,0:T(8,128)S(1)} %get-tuple-element.23.bottom_ref), custom_call_target="tpu_custom_call" | custom-call | tf_op jit(solution)/shard_map/serve/pallas_call | solution.py:183
  25.6 12.0 %all_to_all.10.refs_0_ = bf16[16,8,864]{2,1,0:T(8,128)(2,1)S(1)} all-to-all(bf16[16,8,864]{2,1,0:T(8,128)(2,1)S(1)} %get-tuple-element.25), channel_id=1, replica_groups=mesh['node'=2,'dp'=16] {'dp'}, dimensions={0} | all-to-all | bytes 442368 | tf_op jit(solution)/shard_map/all_to_all | solution.py:189
  37.7 0.0 collective-permute-start.1
  37.7 1.5 %collective-permute-done.1.refs_1_ = bf16[16,8,864]{2,1,0:T(8,128)(2,1)S(1)} collective-permute-done((bf16[16,8,864]{2,1,0:T(8,128)(2,1)S(1)}, bf16[16,8,864]{2,1,0:T(8,128)(2,1)S(1)}, u32[]{:S(2)}, u32[]{:S(2)}) %collective-permute-start.1) | collective-permute-done | bytes 221216 | tf_op jit(solution)/shard_map/ppermute | solution.py:142
  39.1 0.9 %assemble.1 = bf16[16,13824]{1,0:T(8,128)(2,1)} custom-call(bf16[16,8,864]{2,1,0:T(8,128)(2,1)S(1)} %all_to_all.10.refs_0_, bf16[16,8,864]{2,1,0:T(8,128)(2,1)S(1)} %collective-permute-done.1.refs_1_), custom_call_target="tpu_custom_call" | custom-call | tf_op jit(solution)/shard_map/assemble/pallas_call | solution.py:192
Async XLA Ops:
  0.6 5.3 %copy-start = (f32[1,8,13824]{2,1,0:T(8,128)S(1)}, f32[1,8,13824]{2,1,0:T(8,128)}, u32[]{:S(2)}) copy-start(f32[1,8,13824]{2,1,0:T(8,128)} %param.10) | copy-start | bytes 1327108
  0.6 24.2 %copy-start.1 = (f32[8,864]{1,0:T(8,128)S(1)}, f32[8,864]{1,0:T(8,128)}, u32[]{:S(2)}) copy-start(f32[8,864]{1,0:T(8,128)} %error_ref.1) | copy-start | bytes 82948
  3.9 2.0 %collective-permute-start = (f32[8,13824]{1,0:T(8,128)S(1)}, f32[8,13824]{1,0:T(8,128)S(1)}, u32[]{:S(2)}, u32[]{:S(2)}) collective-permute-start(f32[8,13824]{1,0:T(8,128)S(1)} %bitcast.10), channel_id=1, source_target_pairs={{0,16},{16,0},{1,17},{17,1},{2,18},{18,2},{3,19},{19,3},{4,20},{20... | collective-permute-start | bytes 1327112 | tf_op jit(solution)/shard_map/ppermute | solution.py:142
  7.1 17.8 %all-to-all-start = ((bf16[16,8,864]{2,1,0:T(8,128)(2,1)}), bf16[16,8,864]{2,1,0:T(8,128)(2,1)S(1)}, u32[]{:S(2)}, u32[]{:S(2)}) async-start(bf16[16,8,864]{2,1,0:T(8,128)(2,1)} %get-tuple-element.21), calls=%async_computation | async-start | bytes 458752 | tf_op jit(solution)/shard_map/all_to_all | solution.py:172
  37.7 1.5 %collective-permute-start.1 = (bf16[16,8,864]{2,1,0:T(8,128)(2,1)S(1)}, bf16[16,8,864]{2,1,0:T(8,128)(2,1)S(1)}, u32[]{:S(2)}, u32[]{:S(2)}) collective-permute-start(bf16[16,8,864]{2,1,0:T(8,128)(2,1)S(1)} %all_to_all.10.refs_0_), channel_id=1, source_target_pairs={{0,16},{16,0},{1,17},{17,1},{2,18},{18,2},{3,19},{19,3},{4,20},{20... | collective-permute-start | bytes 663560 | tf_op jit(solution)/shard_map/ppermute | solution.py:142

commit v3 on v2

v3 whole, which is shorter than its diff:
```python
import functools

import jax
import jax.numpy as jnp
from jax import lax
from jax.experimental import pallas as pl
from jax.experimental.pallas import tpu as pltpu
from jax.sharding import PartitionSpec as P

beta_one = 0.9
epsilon = 1e-06
learn_rate = 0.5
LANES = 128

VMEM = pl.BlockSpec(memory_space=pltpu.VMEM)
HBM = pl.BlockSpec(memory_space=pltpu.HBM)
MIB = 2**20


def near(*values):
    return [pltpu.with_memory_space_constraint(v, pltpu.VMEM) for v in values]


def far(*values):
    return [pltpu.with_memory_space_constraint(v, pltpu.HBM) for v in values]


def cut(cols):
    if cols % (3 * LANES):
        return [pl.ds(0, cols)]
    first = cols // 3 * 2
    return [pl.ds(0, first), pl.ds(first, cols - first)]


def gradient_kernel(
    cotan_hbm, momentum_hbm, master_hbm, second_hbm, acts_hbm,
    base_ref, theirs_ref, master_ref, bottom_ref,
    cotan_ref, acts, window, sems, cotan_sem, base_sem, master_sem, second_sem,
):
    rows = cotan_ref.shape[0]
    own = base_ref.shape[0]
    width, span, cols = master_ref.shape[1], window.shape[2], master_hbm.shape[1]
    column = lax.axis_index("dp") * width
    start = jnp.minimum((column // LANES) * LANES, cols - span)
    here = pl.ds(pl.multiple_of(start, LANES), span)
    spans = cut(cols)
    cotan_copy = pltpu.make_async_copy(cotan_hbm, cotan_ref, cotan_sem)
    master_copy = pltpu.make_async_copy(master_hbm.at[:, here], window.at[0], master_sem)
    second_copy = pltpu.make_async_copy(second_hbm.at[:, here], window.at[1], second_sem)
    base_copy = pltpu.make_async_copy(momentum_hbm, base_ref, base_sem)
    copies = [pltpu.make_async_copy(acts_hbm.at[:, s], acts.at[:, s], sems.at[i]) for i, s in enumerate(spans)]
    cotan_copy.start()
    copies[0].start()
    master_copy.start()
    second_copy.start()
    base_copy.start()
    for copy in copies[1:]:
        copy.start()
    shift = lax.rem(rows - lax.axis_index("node") * own, rows)
    cotan_copy.wait()
    cotan = pltpu.roll(cotan_ref[...].astype(jnp.float32), shift, 0).astype(jnp.bfloat16)
    shift = lax.rem(span - (column - start), span)
    master_copy.wait()
    second_copy.wait()
    master_ref[...] = pltpu.roll(window[0], shift, 1)[:, :width]
    bottom_ref[...] = jnp.sqrt(pltpu.roll(window[1], shift, 1)[:, :width]) + 1e-08
    for i, (copy, s) in enumerate(zip(copies, spans)):
        copy.wait()
        if i == 0:
            base_copy.wait()
        sums = jnp.dot(cotan, acts[:, s], preferred_element_type=jnp.float32)
        base_ref[:, s] = beta_one * base_ref[:, s] + (1.0 - beta_one) * sums[:own]
        for k in range(theirs_ref.shape[0]):
            theirs_ref[k, :, s] = sums[(k + 1) * own : (k + 2) * own]


def moment_of(base_ref, arrived_refs):
    rest = arrived_refs[0][...]
    for ref in arrived_refs[1:]:
        rest = rest + ref[...]
    return base_ref[...] + (1.0 - beta_one) * rest


def compress(values):
    scale = jnp.sqrt(jnp.mean(values * values, keepdims=True) + epsilon)
    return (scale * jnp.tanh(values / scale)).astype(jnp.bfloat16)


def send_kernel(order, error_ref, base_ref, *refs):
    arrived_refs, (blocks_ref, moment_ref, new_error_ref) = refs[:-3], refs[-3:]
    moment = moment_of(base_ref, arrived_refs)
    moment_ref[...] = moment
    carried = moment + error_ref[...]
    sent = compress(carried)
    new_error_ref[...] = carried - sent.astype(jnp.float32)
    width = blocks_ref.shape[2]
    for place, i in enumerate(order):
        blocks_ref[place] = sent[:, i * width : (i + 1) * width]


def serve_kernel(blocks_ref, error_ref, master_ref, bottom_ref, new_error_ref, out_ref):
    replicas = blocks_ref.shape[0]
    total = blocks_ref[0].astype(jnp.float32)
    for i in range(1, replicas):
        total = total + blocks_ref[i].astype(jnp.float32)
    served = total / replicas + error_ref[...]
    returned = compress(served).astype(jnp.float32)
    new_error_ref[...] = served - returned
    weights = (master_ref[...] - learn_rate * (returned / bottom_ref[...])).astype(jnp.bfloat16)
    for i in range(replicas):
        out_ref[i] = weights


def keep_kernel(*refs):
    *kept, _ = refs[: len(refs) // 2 + 1]
    for source, target in zip(kept, refs[len(kept) + 1 :]):
        target[...] = source[...]


def assemble_kernel(order, *refs):
    parts, (out_hbm, out, sems) = refs[:-3], refs[-3:]
    nodes = len(parts)
    servers, own, width = parts[0].shape
    groups = sems.shape[0]
    each = servers // groups
    me = lax.axis_index("node")
    copies = []
    for i in range(servers):
        loaded = [part[order.index(i)].astype(jnp.float32) for part in parts]
        stacked = []
        for node in range(nodes):
            chosen = loaded[0]
            for k in range(1, nodes):
                chosen = jnp.where(lax.rem(me - k + nodes, nodes) == node, loaded[k], chosen)
            stacked.append(chosen)
        out[:, i * width : (i + 1) * width] = jnp.concatenate(stacked, axis=0).astype(jnp.bfloat16)
        if (i + 1) % each == 0:
            group = i // each
            s = pl.ds(group * each * width, each * width)
            copies.append(pltpu.make_async_copy(out.at[:, s], out_hbm.at[:, s], sems.at[group]))
            copies[-1].start()
    for copy in copies:
        copy.wait()


def ordered(count):
    lead = count // 2 + count // 8
    return [(lead + i) % count for i in range(count)]


def body(hidden, cotangent, momentum, worker_error, server_error, master, second_moment):
    f32, bf16 = jnp.float32, jnp.bfloat16
    nodes, servers = lax.axis_size("node"), lax.axis_size("dp")
    tokens, cols = hidden.shape[1:]
    rows, own = cotangent.shape[2], momentum.shape[1]
    width = cols // servers
    shape = jax.ShapeDtypeStruct

    def exchange(blocks):
        return lax.all_to_all(blocks, "dp", split_axis=0, concat_axis=0, axis_index_groups=[order], tiled=True)

    order = ordered(servers)

    def turn(value, k):
        return lax.ppermute(value, "node", [(i, (i + k) % nodes) for i in range(nodes)])

    def call(kernel, name, outs, in_specs, scratch=(), out_specs=None):
        return pl.pallas_call(
            kernel,
            name=name,
            out_shape=outs,
            in_specs=in_specs,
            out_specs=out_specs or jax.tree.map(lambda _: VMEM, outs),
            scratch_shapes=scratch,
            compiler_params=pltpu.CompilerParams(vmem_limit_bytes=16 * MIB),
        )

    dma = pltpu.SemaphoreType.DMA
    span = min(cols, -(-width // LANES) * LANES + LANES)
    base, theirs, master_part, bottom = call(
        gradient_kernel,
        "gradient",
        (
            pltpu.VMEM((own, cols), f32),
            pltpu.VMEM((nodes - 1, own, cols), f32),
            pltpu.VMEM((own, width), f32),
            pltpu.VMEM((own, width), f32),
        ),
        [HBM] * 5,
        [pltpu.VMEM((rows, tokens), bf16), pltpu.VMEM((tokens, cols), bf16), pltpu.VMEM((2, own, span), f32)]
        + [dma((len(cut(cols)),))] + [dma(())] * 4,
    )(*far(cotangent[0].T, momentum[0], master, second_moment, hidden[0]))
    arrived = [turn(theirs[k - 1], k) for k in range(1, nodes)]

    blocks, moment, new_worker = call(
        functools.partial(send_kernel, order),
        "send",
        (pltpu.VMEM((servers, own, width), bf16), pltpu.VMEM((own, cols), f32), pltpu.VMEM((own, cols), f32)),
        [VMEM] * (2 + len(arrived)),
    )(*near(worker_error[0], base, *arrived))
    gathered = exchange(blocks)

    new_server, copies = call(
        serve_kernel,
        "serve",
        (pltpu.VMEM((own, width), f32), pltpu.VMEM((servers, own, width), bf16)),
        [VMEM] * 4,
    )(*near(gathered, server_error, master_part, bottom))
    everyone = exchange(copies)
    parts = [everyone] + [turn(everyone, k) for k in range(1, nodes)]

    kept = near(moment, new_worker, new_server, everyone)
    moment, new_worker, new_server = call(
        keep_kernel, "keep", tuple(shape(v.shape, f32) for v in kept[:3]), [VMEM] * 4
    )(*kept)

    groups = 2 if servers % 2 == 0 and cols % (2 * LANES) == 0 else 1
    weights = call(
        functools.partial(assemble_kernel, order),
        "assemble",
        shape((rows, cols), bf16),
        [VMEM] * nodes,
        [pltpu.VMEM((rows, cols), bf16), dma((groups,))],
        HBM,
    )(*near(*parts))
    return (moment[None], new_worker[None], new_server, weights)


def solution(mesh):
    placed = (
        P("dp", "node", None),
        P("dp", "node", None),
        P("dp", "node", None),
        P("dp", "node", None),
        P("node", "dp"),
        P("node", None),
        P("node", None),
    )
    return jax.shard_map(
        body,
        mesh=mesh,
        in_specs=placed,
        out_specs=(P("dp", "node", None), P("dp", "node", None), P("node", "dp"), P()),
        check_vma=False,
    )
```

time: 40.4 us -> 34.1 us (0.84)
  blocking collectives: 12 us -> 25.6 us
  waiting for transfers between devices: 10.7 us -> 1.94 us
  starting transfers between devices: 8.78 us -> 0.56 us
  Pallas kernels: 7.87 us -> 5.1 us
    all_to_all x1 -> x2, blocking collectives: 12 us -> 25.6 us  [exchange(): lax.all_to_all(blocks, 'dp', split_axis=0, concat_axis=0, axis_index_grou...]
    all_to_all x1 -> x0, starting transfers between devices: 8.22 us -> none  [body(): lax.all_to_all(blocks, 'dp', split_axis=0, concat_axis=0, tiled=True)]
    all_to_all x1 -> x0, waiting for transfers between devices: 7.82 us -> none  [body(): lax.all_to_all(blocks, 'dp', split_axis=0, concat_axis=0, tiled=True)]
    pallas_call x4, Pallas kernels: 4.62 us -> 2.57 us  [the longest x1 0.97 us: body(): call(keep_kernel, 'keep', tuple((shape(v.shape, f32) for v in kept[:3])),...]
    ppermute x2, waiting for transfers between devices: 2.91 us -> 1.94 us  [turn(): lax.ppermute(value, 'node', [(i, (i + k) % nodes) for i in range(nodes)])]
    pallas_call x1, Pallas kernels: 3.25 us -> 2.54 us  [body(): call(gradient_kernel, 'gradient', (pltpu.VMEM((own, cols), f32), pltpu.VM...]
  transfers between devices with their start and end apart: 3 -> 2, of which waited for: 3 -> 2; matrix products, arithmetic and copies ran while one was open for 0% -> 0% of each run, Pallas kernels for 4% -> 3%
where the time goes in v3:
time: 34.1 us; the launch traced here: 33.9 us
  blocking collectives  25.6 us (75%)
  Pallas kernels  5.1 us (15%)
  waiting for transfers between devices  1.94 us (6%)
  between operations  0.68 us (2%)
  starting transfers between devices  0.56 us (2%)
    all_to_all x2, blocking collectives, exchange(): lax.all_to_all(blocks, 'dp', split_axis=0, concat_axis=0, axis_index_grou...  25.6 us
    pallas_call x1, Pallas kernels, body(): call(gradient_kernel, 'gradient', (pltpu.VMEM((own, cols), f32), pltpu.VM...  2.54 us
    ppermute x2, waiting for transfers between devices, turn(): lax.ppermute(value, 'node', [(i, (i + k) % nodes) for i in range(nodes)])  1.94 us
    pallas_call x1, Pallas kernels, body(): call(keep_kernel, 'keep', tuple((shape(v.shape, f32) for v in kept[:3])),...  0.97 us
    pallas_call x1, Pallas kernels, body(): call(functools.partial(assemble_kernel, order), 'assemble', shape((rows,...  0.91 us
  transfers between devices with their start and end apart: 2, of which 2 were waited for; matrix products, arithmetic and copies ran while one was open for 0% of the time, Pallas kernels for 3%

profile of v3, /device:TPU:0, one launch (start us, length us, event | category | flops | bytes accessed | tf_op | source)
XLA Modules:
  0.0 33.9 jit_solution(12350685068557390380)
XLA Ops:
  0.6 0.0 copy-start
  0.6 0.0 copy-start.1
  0.7 2.5 %gradient.1 = (f32[8,13824]{1,0:T(8,128)S(1)}, f32[1,8,13824]{2,1,0:T(8,128)S(1)}, f32[8,864]{1,0:T(8,128)S(1)}, f32[8,864]{1,0:T(8,128)S(1)}) custom-call(bf16[16,128]{1,0:T(8,128)(2,1)} %bitcast.13, f32[8,13824]{1,0:T(8,128)} %bitcast.12, f32[8,13824]{1,0:T(8,128)} %master_hbm.1, f32[8,13824]{1,0:T(8,128)} %second_hbm.1, bf16[128,13824]{1,0:T(8,128)(2,1)} %bitcast.11), custom_call_target="tpu_custom_call" | custom-call | tf_op jit(solution)/shard_map/gradient/pallas_call | solution.py:180
  3.2 0.6 %collective-permute-start = (f32[8,13824]{1,0:T(8,128)S(1)}, f32[8,13824]{1,0:T(8,128)S(1)}, u32[]{:S(2)}, u32[]{:S(2)}) collective-permute-start(f32[8,13824]{1,0:T(8,128)S(1)} %bitcast.10), channel_id=1, source_target_pairs={{0,16},{16,0},{1,17},{17,1},{2,18},{18,2},{3,19},{19,3},{4,20},{20... | collective-permute-start | bytes 1327112 | tf_op jit(solution)/shard_map/ppermute | solution.py:165
  3.8 1.4 %collective-permute-done.refs_0_ = f32[8,13824]{1,0:T(8,128)S(1)} collective-permute-done((f32[8,13824]{1,0:T(8,128)S(1)}, f32[8,13824]{1,0:T(8,128)S(1)}, u32[]{:S(2)}, u32[]{:S(2)}) %collective-permute-start) | collective-permute-done | bytes 442400 | tf_op jit(solution)/shard_map/ppermute | solution.py:165
  5.2 0.0 copy-done
  5.2 0.5 %send.1 = (bf16[16,8,864]{2,1,0:T(8,128)(2,1)S(1)}, f32[8,13824]{1,0:T(8,128)S(1)}, f32[8,13824]{1,0:T(8,128)S(1)}) custom-call(f32[8,13824]{1,0:T(8,128)S(1)} %bitcast.9, f32[8,13824]{1,0:T(8,128)S(1)} %get-tuple-element.16.base_ref, f32[8,13824]{1,0:T(8,128)S(1)} %collective-permute-done.refs_0_), custom_call_target="tpu_custom_call" | custom-call | tf_op jit(solution)/shard_map/send/pallas_call | solution.py:195
  5.7 15.0 %all_to_all.10.blocks_ref = bf16[16,8,864]{2,1,0:T(8,128)(2,1)S(1)} all-to-all(bf16[16,8,864]{2,1,0:T(8,128)(2,1)S(1)} %get-tuple-element.20), channel_id=1, replica_groups={{10,11,12,13,14,15,0,1,2,3,4,5,6,7,8,9},{26,27,28,29,30,31,16,17,18,19,..., dimensions={0} | all-to-all | bytes 442368 | tf_op jit(solution)/shard_map/all_to_all | solution.py:160
  20.7 0.0 copy-done.1
  20.7 0.2 serve.1
  20.9 10.5 %all_to_all.11.refs_3_.refs_0_ = bf16[16,8,864]{2,1,0:T(8,128)(2,1)S(1)} all-to-all(bf16[16,8,864]{2,1,0:T(8,128)(2,1)S(1)} %get-tuple-element.24), channel_id=1, replica_groups={{10,11,12,13,14,15,0,1,2,3,4,5,6,7,8,9},{26,27,28,29,30,31,16,17,18,19,..., dimensions={0} | all-to-all | bytes 442368 | tf_op jit(solution)/shard_map/all_to_all | solution.py:160
  31.5 0.0 collective-permute-start.1
  31.5 1.0 %keep.1 = (f32[8,13824]{1,0:T(8,128)}, f32[8,13824]{1,0:T(8,128)}, f32[8,864]{1,0:T(8,128)}) custom-call(f32[8,13824]{1,0:T(8,128)S(1)} %get-tuple-element.18.refs_0_, f32[8,13824]{1,0:T(8,128)S(1)} %get-tuple-element.19.refs_1_, f32[8,864]{1,0:T(8,128)S(1)} %get-tuple-element.23.refs_2_, bf16[16,8,864]{2,1,0:T(8,128)(2,1)S(1)} %all_to_all.11.refs_3_.refs_0_), custom_call_target="tpu_custom_call" | custom-call | tf_op jit(solution)/shard_map/keep/pallas_call | solution.py:213
  32.4 0.5 %collective-permute-done.1.refs_1_ = bf16[16,8,864]{2,1,0:T(8,128)(2,1)S(1)} collective-permute-done((bf16[16,8,864]{2,1,0:T(8,128)(2,1)S(1)}, bf16[16,8,864]{2,1,0:T(8,128)(2,1)S(1)}, u32[]{:S(2)}, u32[]{:S(2)}) %collective-permute-start.1) | collective-permute-done | bytes 221216 | tf_op jit(solution)/shard_map/ppermute | solution.py:165
  33.0 0.9 %assemble.1 = bf16[16,13824]{1,0:T(8,128)(2,1)} custom-call(bf16[16,8,864]{2,1,0:T(8,128)(2,1)S(1)} %all_to_all.11.refs_3_.refs_0_, bf16[16,8,864]{2,1,0:T(8,128)(2,1)S(1)} %collective-permute-done.1.refs_1_), custom_call_target="tpu_custom_call" | custom-call | tf_op jit(solution)/shard_map/assemble/pallas_call | solution.py:218
Async XLA Ops:
  0.6 4.5 %copy-start = (f32[1,8,13824]{2,1,0:T(8,128)S(1)}, f32[1,8,13824]{2,1,0:T(8,128)}, u32[]{:S(2)}) copy-start(f32[1,8,13824]{2,1,0:T(8,128)} %param.10) | copy-start | bytes 1327108
  0.6 20.1 %copy-start.1 = (f32[8,864]{1,0:T(8,128)S(1)}, f32[8,864]{1,0:T(8,128)}, u32[]{:S(2)}) copy-start(f32[8,864]{1,0:T(8,128)} %error_ref.1) | copy-start | bytes 82948
  3.2 2.0 %collective-permute-start = (f32[8,13824]{1,0:T(8,128)S(1)}, f32[8,13824]{1,0:T(8,128)S(1)}, u32[]{:S(2)}, u32[]{:S(2)}) collective-permute-start(f32[8,13824]{1,0:T(8,128)S(1)} %bitcast.10), channel_id=1, source_target_pairs={{0,16},{16,0},{1,17},{17,1},{2,18},{18,2},{3,19},{19,3},{4,20},{20... | collective-permute-start | bytes 1327112 | tf_op jit(solution)/shard_map/ppermute | solution.py:165
  31.5 1.5 %collective-permute-start.1 = (bf16[16,8,864]{2,1,0:T(8,128)(2,1)S(1)}, bf16[16,8,864]{2,1,0:T(8,128)(2,1)S(1)}, u32[]{:S(2)}, u32[]{:S(2)}) collective-permute-start(bf16[16,8,864]{2,1,0:T(8,128)(2,1)S(1)} %all_to_all.11.refs_3_.refs_0_), channel_id=1, source_target_pairs={{0,16},{16,0},{1,17},{17,1},{2,18},{18,2},{3,19},{19,3},{4,20},{20... | collective-permute-start | bytes 663560 | tf_op jit(solution)/shard_map/ppermute | solution.py:165

commit v4 on v3

--- a/solution.py
+++ b/solution.py
@@ -111,41 +111,41 @@
         out_ref[i] = weights
 
 
-def keep_kernel(*refs):
-    *kept, _ = refs[: len(refs) // 2 + 1]
-    for source, target in zip(kept, refs[len(kept) + 1 :]):
-        target[...] = source[...]
+def lay_out(order, blocks_ref, rows_ref):
+    width = blocks_ref.shape[2]
+    for i in range(len(order)):
+        rows_ref[:, i * width : (i + 1) * width] = blocks_ref[order.index(i)]
+
+
+def keep_kernel(order, moment_ref, error_ref, server_ref, blocks_ref, moment_hbm, error_hbm, server_hbm, weights_hbm, rows, sems):
+    pairs = [(moment_ref, moment_hbm), (error_ref, error_hbm), (server_ref, server_hbm)]
+    copies = [pltpu.make_async_copy(source, target, sems.at[i]) for i, (source, target) in enumerate(pairs)]
+    for copy in copies:
+        copy.start()
+    lay_out(order, blocks_ref, rows)
+    copies.append(pltpu.make_async_copy(rows, weights_hbm.at[lax.axis_index("node")], sems.at[len(pairs)]))
+    copies[-1].start()
+    for copy in copies:
+        copy.wait()
 
 
 def assemble_kernel(order, *refs):
-    parts, (out_hbm, out, sems) = refs[:-3], refs[-3:]
-    nodes = len(parts)
-    servers, own, width = parts[0].shape
-    groups = sems.shape[0]
-    each = servers // groups
+    *parts, _, out_hbm, rows, sems = refs
+    nodes = out_hbm.shape[0]
     me = lax.axis_index("node")
     copies = []
-    for i in range(servers):
-        loaded = [part[order.index(i)].astype(jnp.float32) for part in parts]
-        stacked = []
-        for node in range(nodes):
-            chosen = loaded[0]
-            for k in range(1, nodes):
-                chosen = jnp.where(lax.rem(me - k + nodes, nodes) == node, loaded[k], chosen)
-            stacked.append(chosen)
-        out[:, i * width : (i + 1) * width] = jnp.concatenate(stacked, axis=0).astype(jnp.bfloat16)
-        if (i + 1) % each == 0:
-            group = i // each
-            s = pl.ds(group * each * width, each * width)
-            copies.append(pltpu.make_async_copy(out.at[:, s], out_hbm.at[:, s], sems.at[group]))
-            copies[-1].start()
+    for k, part in enumerate(parts):
+        lay_out(order, part, rows.at[k])
+        sender = lax.rem(me - (k + 1) + nodes, nodes)
+        copies.append(pltpu.make_async_copy(rows.at[k], out_hbm.at[sender], sems.at[k]))
+        copies[-1].start()
     for copy in copies:
         copy.wait()
 
 
 def ordered(count):
-    lead = count // 2 + count // 8
-    return [(lead + i) % count for i in range(count)]
+    lead = count // 2 + count // 4 - 1
+    return [lead ^ i if count & (count - 1) == 0 else (lead - i) % count for i in range(count)]
 
 
 def body(hidden, cotangent, momentum, worker_error, server_error, master, second_moment):
@@ -164,7 +164,7 @@
     def turn(value, k):
         return lax.ppermute(value, "node", [(i, (i + k) % nodes) for i in range(nodes)])
 
-    def call(kernel, name, outs, in_specs, scratch=(), out_specs=None):
+    def call(kernel, name, outs, in_specs, scratch=(), out_specs=None, aliases={}):
         return pl.pallas_call(
             kernel,
             name=name,
@@ -172,6 +172,7 @@
             in_specs=in_specs,
             out_specs=out_specs or jax.tree.map(lambda _: VMEM, outs),
             scratch_shapes=scratch,
+            input_output_aliases=aliases,
             compiler_params=pltpu.CompilerParams(vmem_limit_bytes=16 * MIB),
         )
 
@@ -207,22 +208,27 @@
         [VMEM] * 4,
     )(*near(gathered, server_error, master_part, bottom))
     everyone = exchange(copies)
-    parts = [everyone] + [turn(everyone, k) for k in range(1, nodes)]
-
-    kept = near(moment, new_worker, new_server, everyone)
-    moment, new_worker, new_server = call(
-        keep_kernel, "keep", tuple(shape(v.shape, f32) for v in kept[:3]), [VMEM] * 4
-    )(*kept)
-
-    groups = 2 if servers % 2 == 0 and cols % (2 * LANES) == 0 else 1
+    others = [turn(everyone, k) for k in range(1, nodes)]
+
+    whole = (nodes, own, cols)
+    moment, new_worker, new_server, weights = call(
+        functools.partial(keep_kernel, order),
+        "keep",
+        (*(shape(v.shape, f32) for v in (moment, new_worker, new_server)), shape(whole, bf16)),
+        [VMEM] * 4,
+        [pltpu.VMEM((own, cols), bf16), dma((4,))],
+        (HBM,) * 4,
+    )(*near(moment, new_worker, new_server, everyone))
     weights = call(
         functools.partial(assemble_kernel, order),
         "assemble",
-        shape((rows, cols), bf16),
-        [VMEM] * nodes,
-        [pltpu.VMEM((rows, cols), bf16), dma((groups,))],
+        shape(whole, bf16),
+        [VMEM] * len(others) + [HBM],
+        [pltpu.VMEM((nodes - 1, own, cols), bf16), dma((nodes - 1,))],
         HBM,
-    )(*near(*parts))
+        {len(others): 0},
+    )(*near(*others), weights)
+    weights = weights.reshape(rows, cols)
     return (moment[None], new_worker[None], new_server, weights)
 
 

time: 34.1 us -> 33.3 us (0.977)
  blocking collectives: 25.6 us -> 24.9 us
    all_to_all x2, blocking collectives: 25.6 us -> 24.9 us  [exchange(): lax.all_to_all(blocks, 'dp', split_axis=0, concat_axis=0, axis_index_grou...]
where the time goes in v4:
time: 33.3 us; the launch traced here: 33.1 us
  blocking collectives  24.9 us (75%)
  Pallas kernels  5.07 us (15%)
  waiting for transfers between devices  1.88 us (6%)
  between operations  0.68 us (2%)
  starting transfers between devices  0.56 us (2%)
    all_to_all x2, blocking collectives, exchange(): lax.all_to_all(blocks, 'dp', split_axis=0, concat_axis=0, axis_index_grou...  24.9 us
    pallas_call x1, Pallas kernels, body(): call(gradient_kernel, 'gradient', (pltpu.VMEM((own, cols), f32), pltpu.VM...  2.54 us
    ppermute x2, waiting for transfers between devices, turn(): lax.ppermute(value, 'node', [(i, (i + k) % nodes) for i in range(nodes)])  1.88 us
    pallas_call x1, Pallas kernels, body(): call(functools.partial(keep_kernel, order), 'keep', (*(shape(v.shape, f32...  1.02 us
    pallas_call x1, Pallas kernels, body(): call(functools.partial(assemble_kernel, order), 'assemble', shape(whole,...  0.81 us
  transfers between devices with their start and end apart: 2, of which 2 were waited for; matrix products, arithmetic and copies ran while one was open for 0% of the time, Pallas kernels for 3%

profile of v4, /device:TPU:0, one launch (start us, length us, event | category | flops | bytes accessed | tf_op | source)
XLA Modules:
  0.0 33.1 jit_solution(1984318478020244147)
XLA Ops:
  0.6 0.0 copy-start
  0.6 0.0 copy-start.1
  0.7 2.5 %gradient.1 = (f32[8,13824]{1,0:T(8,128)S(1)}, f32[1,8,13824]{2,1,0:T(8,128)S(1)}, f32[8,864]{1,0:T(8,128)S(1)}, f32[8,864]{1,0:T(8,128)S(1)}) custom-call(bf16[16,128]{1,0:T(8,128)(2,1)} %bitcast.15, f32[8,13824]{1,0:T(8,128)} %bitcast.14, f32[8,13824]{1,0:T(8,128)} %master_hbm.1, f32[8,13824]{1,0:T(8,128)} %second_hbm.1, bf16[128,13824]{1,0:T(8,128)(2,1)} %bitcast.12), custom_call_target="tpu_custom_call" | custom-call | tf_op jit(solution)/shard_map/gradient/pallas_call | solution.py:181
  3.2 0.6 %collective-permute-start = (f32[8,13824]{1,0:T(8,128)S(1)}, f32[8,13824]{1,0:T(8,128)S(1)}, u32[]{:S(2)}, u32[]{:S(2)}) collective-permute-start(f32[8,13824]{1,0:T(8,128)S(1)} %bitcast.11), channel_id=1, source_target_pairs={{0,16},{16,0},{1,17},{17,1},{2,18},{18,2},{3,19},{19,3},{4,20},{20... | collective-permute-start | bytes 1327112 | tf_op jit(solution)/shard_map/ppermute | solution.py:165
  3.8 1.4 %collective-permute-done.refs_0_ = f32[8,13824]{1,0:T(8,128)S(1)} collective-permute-done((f32[8,13824]{1,0:T(8,128)S(1)}, f32[8,13824]{1,0:T(8,128)S(1)}, u32[]{:S(2)}, u32[]{:S(2)}) %collective-permute-start) | collective-permute-done | bytes 442400 | tf_op jit(solution)/shard_map/ppermute | solution.py:165
  5.2 0.0 copy-done
  5.2 0.5 %send.1 = (bf16[16,8,864]{2,1,0:T(8,128)(2,1)S(1)}, f32[8,13824]{1,0:T(8,128)S(1)}, f32[8,13824]{1,0:T(8,128)S(1)}) custom-call(f32[8,13824]{1,0:T(8,128)S(1)} %bitcast.10, f32[8,13824]{1,0:T(8,128)S(1)} %get-tuple-element.17.base_ref, f32[8,13824]{1,0:T(8,128)S(1)} %collective-permute-done.refs_0_), custom_call_target="tpu_custom_call" | custom-call | tf_op jit(solution)/shard_map/send/pallas_call | solution.py:196
  5.7 14.2 %all_to_all.10.blocks_ref = bf16[16,8,864]{2,1,0:T(8,128)(2,1)S(1)} all-to-all(bf16[16,8,864]{2,1,0:T(8,128)(2,1)S(1)} %get-tuple-element.21), channel_id=1, replica_groups={{11,10,9,8,15,14,13,12,3,2,1,0,7,6,5,4},{27,26,25,24,31,30,29,28,19,18,..., dimensions={0} | all-to-all | bytes 442368 | tf_op jit(solution)/shard_map/all_to_all | solution.py:160
  19.9 0.0 copy-done.1
  19.9 0.2 serve.1
  20.1 10.8 %all_to_all.11.blocks_ref = bf16[16,8,864]{2,1,0:T(8,128)(2,1)S(1)} all-to-all(bf16[16,8,864]{2,1,0:T(8,128)(2,1)S(1)} %get-tuple-element.25), channel_id=1, replica_groups={{11,10,9,8,15,14,13,12,3,2,1,0,7,6,5,4},{27,26,25,24,31,30,29,28,19,18,..., dimensions={0} | all-to-all | bytes 442368 | tf_op jit(solution)/shard_map/all_to_all | solution.py:160
  30.8 0.0 collective-permute-start.1
  30.8 1.0 %keep.1 = (f32[8,13824]{1,0:T(8,128)}, f32[8,13824]{1,0:T(8,128)}, f32[8,864]{1,0:T(8,128)}, bf16[2,8,13824]{2,1,0:T(8,128)(2,1)}) custom-call(f32[8,13824]{1,0:T(8,128)S(1)} %get-tuple-element.19.moment_ref, f32[8,13824]{1,0:T(8,128)S(1)} %get-tuple-element.20.error_ref, f32[8,864]{1,0:T(8,128)S(1)} %get-tuple-element.24.server_ref, ...), custom_call_target="tpu_custom_call" | custom-call | tf_op jit(solution)/shard_map/keep/pallas_call | solution.py:214
  31.9 0.5 %collective-permute-done.1.refs_0_ = bf16[16,8,864]{2,1,0:T(8,128)(2,1)S(1)} collective-permute-done((bf16[16,8,864]{2,1,0:T(8,128)(2,1)S(1)}, bf16[16,8,864]{2,1,0:T(8,128)(2,1)S(1)}, u32[]{:S(2)}, u32[]{:S(2)}) %collective-permute-start.1) | collective-permute-done | bytes 221216 | tf_op jit(solution)/shard_map/ppermute | solution.py:165
  32.3 0.8 %assemble.1 = bf16[2,8,13824]{2,1,0:T(8,128)(2,1)} custom-call(bf16[16,8,864]{2,1,0:T(8,128)(2,1)S(1)} %collective-permute-done.1.refs_0_, bf16[2,8,13824]{2,1,0:T(8,128)(2,1)} %get-tuple-element.29.refs_1_), custom_call_target="tpu_custom_call", output_to_operand_aliasing={{}: (1, {})} | custom-call | tf_op jit(solution)/shard_map/assemble/pallas_call | solution.py:222
Async XLA Ops:
  0.6 4.5 %copy-start = (f32[1,8,13824]{2,1,0:T(8,128)S(1)}, f32[1,8,13824]{2,1,0:T(8,128)}, u32[]{:S(2)}) copy-start(f32[1,8,13824]{2,1,0:T(8,128)} %param.10) | copy-start | bytes 1327108
  0.6 19.2 %copy-start.1 = (f32[8,864]{1,0:T(8,128)S(1)}, f32[8,864]{1,0:T(8,128)}, u32[]{:S(2)}) copy-start(f32[8,864]{1,0:T(8,128)} %error_ref.1) | copy-start | bytes 82948
  3.2 2.0 %collective-permute-start = (f32[8,13824]{1,0:T(8,128)S(1)}, f32[8,13824]{1,0:T(8,128)S(1)}, u32[]{:S(2)}, u32[]{:S(2)}) collective-permute-start(f32[8,13824]{1,0:T(8,128)S(1)} %bitcast.11), channel_id=1, source_target_pairs={{0,16},{16,0},{1,17},{17,1},{2,18},{18,2},{3,19},{19,3},{4,20},{20... | collective-permute-start | bytes 1327112 | tf_op jit(solution)/shard_map/ppermute | solution.py:165
  30.8 1.5 %collective-permute-start.1 = (bf16[16,8,864]{2,1,0:T(8,128)(2,1)S(1)}, bf16[16,8,864]{2,1,0:T(8,128)(2,1)S(1)}, u32[]{:S(2)}, u32[]{:S(2)}) collective-permute-start(bf16[16,8,864]{2,1,0:T(8,128)(2,1)S(1)} %all_to_all.11.blocks_ref), channel_id=1, source_target_pairs={{0,16},{16,0},{1,17},{17,1},{2,18},{18,2},{3,19},{19,3},{4,20},{20... | collective-permute-start | bytes 663560 | tf_op jit(solution)/shard_map/ppermute | solution.py:165

commit v5 on v4

--- a/solution.py
+++ b/solution.py
@@ -32,46 +32,52 @@
     return [pl.ds(0, first), pl.ds(first, cols - first)]
 
 
-def gradient_kernel(
-    cotan_hbm, momentum_hbm, master_hbm, second_hbm, acts_hbm,
-    base_ref, theirs_ref, master_ref, bottom_ref,
-    cotan_ref, acts, window, sems, cotan_sem, base_sem, master_sem, second_sem,
+def gradient_kernel(cotan_hbm, acts_hbm, mine_ref, theirs_ref, cotan_ref, acts, cotan_sem, sems):
+    rows = cotan_ref.shape[0]
+    own = mine_ref.shape[0]
+    spans = cut(acts.shape[1])
+    cotan_copy = pltpu.make_async_copy(cotan_hbm, cotan_ref, cotan_sem)
+    copies = [pltpu.make_async_copy(acts_hbm.at[:, s], acts.at[:, s], sems.at[i]) for i, s in enumerate(spans)]
+    for copy in [cotan_copy, *copies]:
+        copy.start()
+    shift = lax.rem(rows - lax.axis_index("node") * own, rows)
+    cotan_copy.wait()
+    cotan = pltpu.roll(cotan_ref[...].astype(jnp.float32), shift, 0).astype(jnp.bfloat16)
+    for copy, s in zip(copies, spans):
+        copy.wait()
+        sums = jnp.dot(cotan, acts[:, s], preferred_element_type=jnp.float32)
+        mine_ref[:, s] = sums[:own]
+        for k in range(theirs_ref.shape[0]):
+            theirs_ref[k, :, s] = sums[(k + 1) * own : (k + 2) * own]
+
+
+def prepare_kernel(
+    momentum_hbm, error_hbm, server_hbm, master_hbm, second_hbm, mine_ref,
+    base_ref, error_ref, server_ref, master_ref, bottom_ref, window, sems,
 ):
-    rows = cotan_ref.shape[0]
-    own = base_ref.shape[0]
     width, span, cols = master_ref.shape[1], window.shape[2], master_hbm.shape[1]
     column = lax.axis_index("dp") * width
     start = jnp.minimum((column // LANES) * LANES, cols - span)
     here = pl.ds(pl.multiple_of(start, LANES), span)
-    spans = cut(cols)
-    cotan_copy = pltpu.make_async_copy(cotan_hbm, cotan_ref, cotan_sem)
-    master_copy = pltpu.make_async_copy(master_hbm.at[:, here], window.at[0], master_sem)
-    second_copy = pltpu.make_async_copy(second_hbm.at[:, here], window.at[1], second_sem)
-    base_copy = pltpu.make_async_copy(momentum_hbm, base_ref, base_sem)
-    copies = [pltpu.make_async_copy(acts_hbm.at[:, s], acts.at[:, s], sems.at[i]) for i, s in enumerate(spans)]
-    cotan_copy.start()
-    copies[0].start()
-    master_copy.start()
-    second_copy.start()
-    base_copy.start()
-    for copy in copies[1:]:
+    pairs = [
+        (master_hbm.at[:, here], window.at[0]),
+        (second_hbm.at[:, here], window.at[1]),
+        (server_hbm, server_ref),
+        (momentum_hbm, base_ref),
+        (error_hbm, error_ref),
+    ]
+    copies = [pltpu.make_async_copy(source, target, sems.at[i]) for i, (source, target) in enumerate(pairs)]
+    for copy in copies:
         copy.start()
-    shift = lax.rem(rows - lax.axis_index("node") * own, rows)
-    cotan_copy.wait()
-    cotan = pltpu.roll(cotan_ref[...].astype(jnp.float32), shift, 0).astype(jnp.bfloat16)
     shift = lax.rem(span - (column - start), span)
-    master_copy.wait()
-    second_copy.wait()
+    copies[0].wait()
+    copies[1].wait()
     master_ref[...] = pltpu.roll(window[0], shift, 1)[:, :width]
     bottom_ref[...] = jnp.sqrt(pltpu.roll(window[1], shift, 1)[:, :width]) + 1e-08
-    for i, (copy, s) in enumerate(zip(copies, spans)):
-        copy.wait()
-        if i == 0:
-            base_copy.wait()
-        sums = jnp.dot(cotan, acts[:, s], preferred_element_type=jnp.float32)
-        base_ref[:, s] = beta_one * base_ref[:, s] + (1.0 - beta_one) * sums[:own]
-        for k in range(theirs_ref.shape[0]):
-            theirs_ref[k, :, s] = sums[(k + 1) * own : (k + 2) * own]
+    for copy in copies[2:4]:
+        copy.wait()
+    base_ref[...] = beta_one * base_ref[...] + (1.0 - beta_one) * mine_ref[...]
+    copies[4].wait()
 
 
 def moment_of(base_ref, arrived_refs):
@@ -177,28 +183,30 @@
         )
 
     dma = pltpu.SemaphoreType.DMA
-    span = min(cols, -(-width // LANES) * LANES + LANES)
-    base, theirs, master_part, bottom = call(
+    mine, theirs = call(
         gradient_kernel,
         "gradient",
-        (
-            pltpu.VMEM((own, cols), f32),
-            pltpu.VMEM((nodes - 1, own, cols), f32),
-            pltpu.VMEM((own, width), f32),
-            pltpu.VMEM((own, width), f32),
-        ),
-        [HBM] * 5,
-        [pltpu.VMEM((rows, tokens), bf16), pltpu.VMEM((tokens, cols), bf16), pltpu.VMEM((2, own, span), f32)]
-        + [dma((len(cut(cols)),))] + [dma(())] * 4,
-    )(*far(cotangent[0].T, momentum[0], master, second_moment, hidden[0]))
+        (pltpu.VMEM((own, cols), f32), pltpu.VMEM((nodes - 1, own, cols), f32)),
+        [HBM] * 2,
+        [pltpu.VMEM((rows, tokens), bf16), pltpu.VMEM((tokens, cols), bf16), dma(()), dma((len(cut(cols)),))],
+    )(*far(cotangent[0].T, hidden[0]))
     arrived = [turn(theirs[k - 1], k) for k in range(1, nodes)]
+
+    span = min(cols, -(-width // LANES) * LANES + LANES)
+    base, error, server, master_part, bottom = call(
+        prepare_kernel,
+        "prepare",
+        (pltpu.VMEM((own, cols), f32),) * 2 + (pltpu.VMEM((own, width), f32),) * 3,
+        [HBM] * 5 + [VMEM],
+        [pltpu.VMEM((2, own, span), f32), dma((5,))],
+    )(*far(momentum[0], worker_error[0], server_error, master, second_moment), *near(mine))
 
     blocks, moment, new_worker = call(
         functools.partial(send_kernel, order),
         "send",
         (pltpu.VMEM((servers, own, width), bf16), pltpu.VMEM((own, cols), f32), pltpu.VMEM((own, cols), f32)),
         [VMEM] * (2 + len(arrived)),
-    )(*near(worker_error[0], base, *arrived))
+    )(*near(error, base, *arrived))
     gathered = exchange(blocks)
 
     new_server, copies = call(
@@ -206,7 +214,7 @@
         "serve",
         (pltpu.VMEM((own, width), f32), pltpu.VMEM((servers, own, width), bf16)),
         [VMEM] * 4,
-    )(*near(gathered, server_error, master_part, bottom))
+    )(*near(gathered, server, master_part, bottom))
     everyone = exchange(copies)
     others = [turn(everyone, k) for k in range(1, nodes)]
 

time: 33.3 us -> 33.2 us (level)
  waiting for transfers between devices: 1.88 us -> 0.62 us
  Pallas kernels: 5.07 us -> 6.16 us
    ppermute x2, waiting for transfers between devices: 1.88 us -> 0.62 us  [turn(): lax.ppermute(value, 'node', [(i, (i + k) % nodes) for i in range(nodes)])]
    pallas_call x0 -> x1, Pallas kernels: none -> 1.25 us  [body(): call(prepare_kernel, 'prepare', (pltpu.VMEM((own, cols), f32),) * 2 + (pl...]
  transfers between devices with their start and end apart: 2 -> 2, of which waited for: 2 -> 2; matrix products, arithmetic and copies ran while one was open for 0% -> 0% of each run, Pallas kernels for 3% -> 7%
where the time goes in v5:
time: 33.2 us; the launch traced here: 33 us
  blocking collectives  24.9 us (75%)
  Pallas kernels  6.16 us (19%)
  between operations  0.67 us (2%)
  waiting for transfers between devices  0.62 us (2%)
  starting transfers between devices  0.56 us (2%)
    all_to_all x2, blocking collectives, exchange(): lax.all_to_all(blocks, 'dp', split_axis=0, concat_axis=0, axis_index_grou...  24.9 us
    pallas_call x1, Pallas kernels, body(): call(gradient_kernel, 'gradient', (pltpu.VMEM((own, cols), f32), pltpu.VM...  2.38 us
    pallas_call x1, Pallas kernels, body(): call(prepare_kernel, 'prepare', (pltpu.VMEM((own, cols), f32),) * 2 + (pl...  1.25 us
    pallas_call x1, Pallas kernels, body(): call(functools.partial(keep_kernel, order), 'keep', (*(shape(v.shape, f32...  1.02 us
    pallas_call x1, Pallas kernels, body(): call(functools.partial(assemble_kernel, order), 'assemble', shape(whole,...  0.81 us
  transfers between devices with their start and end apart: 2, of which 2 were waited for; matrix products, arithmetic and copies ran while one was open for 0% of the time, Pallas kernels for 7%

profile of v5, /device:TPU:0, one launch (start us, length us, event | category | flops | bytes accessed | tf_op | source)
XLA Modules:
  0.0 33.0 jit_solution(7959144208209725000)
XLA Ops:
  0.6 2.4 %gradient.1 = (f32[8,13824]{1,0:T(8,128)S(1)}, f32[1,8,13824]{2,1,0:T(8,128)S(1)}) custom-call(bf16[16,128]{1,0:T(8,128)(2,1)} %bitcast.15, bf16[128,13824]{1,0:T(8,128)(2,1)} %bitcast.11), custom_call_target="tpu_custom_call" | custom-call | tf_op jit(solution)/shard_map/gradient/pallas_call | solution.py:186
  3.0 0.6 %collective-permute-start = (f32[8,13824]{1,0:T(8,128)S(1)}, f32[8,13824]{1,0:T(8,128)S(1)}, u32[]{:S(2)}, u32[]{:S(2)}) collective-permute-start(f32[8,13824]{1,0:T(8,128)S(1)} %bitcast.10), channel_id=1, source_target_pairs={{0,16},{16,0},{1,17},{17,1},{2,18},{18,2},{3,19},{19,3},{4,20},{20... | collective-permute-start | bytes 1327112 | tf_op jit(solution)/shard_map/ppermute | solution.py:171
  3.6 1.2 %prepare.1 = (f32[8,13824]{1,0:T(8,128)S(1)}, f32[8,13824]{1,0:T(8,128)S(1)}, f32[8,864]{1,0:T(8,128)S(1)}, f32[8,864]{1,0:T(8,128)S(1)}, f32[8,864]{1,0:T(8,128)S(1)}) custom-call(f32[8,13824]{1,0:T(8,128)} %bitcast.13, f32[8,13824]{1,0:T(8,128)} %bitcast.14, f32[8,864]{1,0:T(8,128)} %server_hbm.1, f32[8,13824]{1,0:T(8,128)} %master_hbm.1, ...), custom_call_target="tpu_custom_call" | custom-call | tf_op jit(solution)/shard_map/prepare/pallas_call | solution.py:196
  4.8 0.2 collective-permute-done.refs_0_
  5.0 0.5 %send.1 = (bf16[16,8,864]{2,1,0:T(8,128)(2,1)S(1)}, f32[8,13824]{1,0:T(8,128)S(1)}, f32[8,13824]{1,0:T(8,128)S(1)}) custom-call(f32[8,13824]{1,0:T(8,128)S(1)} %get-tuple-element.21.error_ref, f32[8,13824]{1,0:T(8,128)S(1)} %get-tuple-element.22.base_ref, f32[8,13824]{1,0:T(8,128)S(1)} %collective-permute-done.refs_0_), custom_call_target="tpu_custom_call" | custom-call | tf_op jit(solution)/shard_map/send/pallas_call | solution.py:204
  5.5 14.2 %all_to_all.10.blocks_ref = bf16[16,8,864]{2,1,0:T(8,128)(2,1)S(1)} all-to-all(bf16[16,8,864]{2,1,0:T(8,128)(2,1)S(1)} %get-tuple-element.26), channel_id=1, replica_groups={{11,10,9,8,15,14,13,12,3,2,1,0,7,6,5,4},{27,26,25,24,31,30,29,28,19,18,..., dimensions={0} | all-to-all | bytes 442368 | tf_op jit(solution)/shard_map/all_to_all | solution.py:166
  19.7 0.2 serve.1
  19.9 10.8 %all_to_all.11.blocks_ref = bf16[16,8,864]{2,1,0:T(8,128)(2,1)S(1)} all-to-all(bf16[16,8,864]{2,1,0:T(8,128)(2,1)S(1)} %get-tuple-element.31), channel_id=1, replica_groups={{11,10,9,8,15,14,13,12,3,2,1,0,7,6,5,4},{27,26,25,24,31,30,29,28,19,18,..., dimensions={0} | all-to-all | bytes 442368 | tf_op jit(solution)/shard_map/all_to_all | solution.py:166
  30.7 0.0 collective-permute-start.1
  30.7 1.0 %keep.1 = (f32[8,13824]{1,0:T(8,128)}, f32[8,13824]{1,0:T(8,128)}, f32[8,864]{1,0:T(8,128)}, bf16[2,8,13824]{2,1,0:T(8,128)(2,1)}) custom-call(f32[8,13824]{1,0:T(8,128)S(1)} %get-tuple-element.24.moment_ref, f32[8,13824]{1,0:T(8,128)S(1)} %get-tuple-element.25.error_ref, f32[8,864]{1,0:T(8,128)S(1)} %get-tuple-element.30.server_ref, ...), custom_call_target="tpu_custom_call" | custom-call | tf_op jit(solution)/shard_map/keep/pallas_call | solution.py:222
  31.7 0.5 %collective-permute-done.1.refs_0_ = bf16[16,8,864]{2,1,0:T(8,128)(2,1)S(1)} collective-permute-done((bf16[16,8,864]{2,1,0:T(8,128)(2,1)S(1)}, bf16[16,8,864]{2,1,0:T(8,128)(2,1)S(1)}, u32[]{:S(2)}, u32[]{:S(2)}) %collective-permute-start.1) | collective-permute-done | bytes 221216 | tf_op jit(solution)/shard_map/ppermute | solution.py:171
  32.1 0.8 %assemble.1 = bf16[2,8,13824]{2,1,0:T(8,128)(2,1)} custom-call(bf16[16,8,864]{2,1,0:T(8,128)(2,1)S(1)} %collective-permute-done.1.refs_0_, bf16[2,8,13824]{2,1,0:T(8,128)(2,1)} %get-tuple-element.35.refs_1_), custom_call_target="tpu_custom_call", output_to_operand_aliasing={{}: (1, {})} | custom-call | tf_op jit(solution)/shard_map/assemble/pallas_call | solution.py:230
Async XLA Ops:
  3.0 2.0 %collective-permute-start = (f32[8,13824]{1,0:T(8,128)S(1)}, f32[8,13824]{1,0:T(8,128)S(1)}, u32[]{:S(2)}, u32[]{:S(2)}) collective-permute-start(f32[8,13824]{1,0:T(8,128)S(1)} %bitcast.10), channel_id=1, source_target_pairs={{0,16},{16,0},{1,17},{17,1},{2,18},{18,2},{3,19},{19,3},{4,20},{20... | collective-permute-start | bytes 1327112 | tf_op jit(solution)/shard_map/ppermute | solution.py:171
  30.7 1.5 %collective-permute-start.1 = (bf16[16,8,864]{2,1,0:T(8,128)(2,1)S(1)}, bf16[16,8,864]{2,1,0:T(8,128)(2,1)S(1)}, u32[]{:S(2)}, u32[]{:S(2)}) collective-permute-start(bf16[16,8,864]{2,1,0:T(8,128)(2,1)S(1)} %all_to_all.11.blocks_ref), channel_id=1, source_target_pairs={{0,16},{16,0},{1,17},{17,1},{2,18},{18,2},{3,19},{19,3},{4,20},{20... | collective-permute-start | bytes 663560 | tf_op jit(solution)/shard_map/ppermute | solution.py:171

commit v6 on v5

--- a/solution.py
+++ b/solution.py
@@ -53,7 +53,7 @@
 
 def prepare_kernel(
     momentum_hbm, error_hbm, server_hbm, master_hbm, second_hbm, mine_ref,
-    base_ref, error_ref, server_ref, master_ref, bottom_ref, window, sems,
+    base_ref, start_ref, server_ref, master_ref, bottom_ref, window, sems,
 ):
     width, span, cols = master_ref.shape[1], window.shape[2], master_hbm.shape[1]
     column = lax.axis_index("dp") * width
@@ -64,7 +64,7 @@
         (second_hbm.at[:, here], window.at[1]),
         (server_hbm, server_ref),
         (momentum_hbm, base_ref),
-        (error_hbm, error_ref),
+        (error_hbm, start_ref),
     ]
     copies = [pltpu.make_async_copy(source, target, sems.at[i]) for i, (source, target) in enumerate(pairs)]
     for copy in copies:
@@ -76,30 +76,40 @@
     bottom_ref[...] = jnp.sqrt(pltpu.roll(window[1], shift, 1)[:, :width]) + 1e-08
     for copy in copies[2:4]:
         copy.wait()
-    base_ref[...] = beta_one * base_ref[...] + (1.0 - beta_one) * mine_ref[...]
+    base = beta_one * base_ref[...] + (1.0 - beta_one) * mine_ref[...]
+    base_ref[...] = base
     copies[4].wait()
-
-
-def moment_of(base_ref, arrived_refs):
-    rest = arrived_refs[0][...]
+    start_ref[...] = base + start_ref[...]
+
+
+def arrived_part(arrived_refs, s):
+    rest = arrived_refs[0][:, s]
     for ref in arrived_refs[1:]:
-        rest = rest + ref[...]
-    return base_ref[...] + (1.0 - beta_one) * rest
-
-
-def compress(values):
-    scale = jnp.sqrt(jnp.mean(values * values, keepdims=True) + epsilon)
+        rest = rest + ref[:, s]
+    return (1.0 - beta_one) * rest
+
+
+def compress(values, squares):
+    scale = jnp.sqrt(squares + epsilon)
     return (scale * jnp.tanh(values / scale)).astype(jnp.bfloat16)
 
 
-def send_kernel(order, error_ref, base_ref, *refs):
-    arrived_refs, (blocks_ref, moment_ref, new_error_ref) = refs[:-3], refs[-3:]
-    moment = moment_of(base_ref, arrived_refs)
-    moment_ref[...] = moment
-    carried = moment + error_ref[...]
-    sent = compress(carried)
-    new_error_ref[...] = carried - sent.astype(jnp.float32)
+def send_kernel(order, start_ref, *refs):
+    arrived_refs, (blocks_ref, sent_ref) = refs[:-2], refs[-2:]
+    rows, cols = start_ref.shape
     width = blocks_ref.shape[2]
+    chunks = piece_count(len(order), width)
+    step = cols // chunks
+
+    def squares(i, total):
+        s = pl.ds(pl.multiple_of(i * step, LANES), step)
+        carried = start_ref[:, s] + arrived_part(arrived_refs, s)
+        return total + carried * carried
+
+    total = lax.fori_loop(0, chunks, squares, jnp.zeros((rows, step), jnp.float32))
+    mean = jnp.sum(total, keepdims=True) / (rows * cols)
+    sent = compress(start_ref[...] + arrived_part(arrived_refs, slice(None)), mean)
+    sent_ref[...] = sent
     for place, i in enumerate(order):
         blocks_ref[place] = sent[:, i * width : (i + 1) * width]
 
@@ -110,7 +120,7 @@
     for i in range(1, replicas):
         total = total + blocks_ref[i].astype(jnp.float32)
     served = total / replicas + error_ref[...]
-    returned = compress(served).astype(jnp.float32)
+    returned = compress(served, jnp.mean(served * served, keepdims=True)).astype(jnp.float32)
     new_error_ref[...] = served - returned
     weights = (master_ref[...] - learn_rate * (returned / bottom_ref[...])).astype(jnp.bfloat16)
     for i in range(replicas):
@@ -123,14 +133,26 @@
         rows_ref[:, i * width : (i + 1) * width] = blocks_ref[order.index(i)]
 
 
-def keep_kernel(order, moment_ref, error_ref, server_ref, blocks_ref, moment_hbm, error_hbm, server_hbm, weights_hbm, rows, sems):
-    pairs = [(moment_ref, moment_hbm), (error_ref, error_hbm), (server_ref, server_hbm)]
-    copies = [pltpu.make_async_copy(source, target, sems.at[i]) for i, (source, target) in enumerate(pairs)]
-    for copy in copies:
-        copy.start()
+def piece_count(servers, width):
+    return max(n for n in (1, 2, 4) if servers % n == 0 and servers // n * width % LANES == 0)
+
+
+def keep_kernel(order, base_ref, start_ref, sent_ref, server_ref, blocks_ref, *refs):
+    *arrived_refs, moment_hbm, error_hbm, server_hbm, weights_hbm, moment, error, rows, sems = refs
+    copies = [
+        pltpu.make_async_copy(server_ref, server_hbm, sems.at[0]),
+        pltpu.make_async_copy(moment, moment_hbm, sems.at[1]),
+        pltpu.make_async_copy(error, error_hbm, sems.at[2]),
+        pltpu.make_async_copy(rows, weights_hbm.at[lax.axis_index("node")], sems.at[3]),
+    ]
+    copies[0].start()
+    rest = arrived_part(arrived_refs, slice(None))
+    moment[...] = base_ref[...] + rest
+    copies[1].start()
+    error[...] = (start_ref[...] + rest) - sent_ref[...].astype(jnp.float32)
+    copies[2].start()
     lay_out(order, blocks_ref, rows)
-    copies.append(pltpu.make_async_copy(rows, weights_hbm.at[lax.axis_index("node")], sems.at[len(pairs)]))
-    copies[-1].start()
+    copies[3].start()
     for copy in copies:
         copy.wait()
 
@@ -193,7 +215,7 @@
     arrived = [turn(theirs[k - 1], k) for k in range(1, nodes)]
 
     span = min(cols, -(-width // LANES) * LANES + LANES)
-    base, error, server, master_part, bottom = call(
+    base, begun, server, master_part, bottom = call(
         prepare_kernel,
         "prepare",
         (pltpu.VMEM((own, cols), f32),) * 2 + (pltpu.VMEM((own, width), f32),) * 3,
@@ -201,12 +223,12 @@
         [pltpu.VMEM((2, own, span), f32), dma((5,))],
     )(*far(momentum[0], worker_error[0], server_error, master, second_moment), *near(mine))
 
-    blocks, moment, new_worker = call(
+    blocks, sent = call(
         functools.partial(send_kernel, order),
         "send",
-        (pltpu.VMEM((servers, own, width), bf16), pltpu.VMEM((own, cols), f32), pltpu.VMEM((own, cols), f32)),
-        [VMEM] * (2 + len(arrived)),
-    )(*near(error, base, *arrived))
+        (pltpu.VMEM((servers, own, width), bf16), pltpu.VMEM((own, cols), bf16)),
+        [VMEM] * (1 + len(arrived)),
+    )(*near(begun, *arrived))
     gathered = exchange(blocks)
 
     new_server, copies = call(
@@ -222,11 +244,11 @@
     moment, new_worker, new_server, weights = call(
         functools.partial(keep_kernel, order),
         "keep",
-        (*(shape(v.shape, f32) for v in (moment, new_worker, new_server)), shape(whole, bf16)),
-        [VMEM] * 4,
-        [pltpu.VMEM((own, cols), bf16), dma((4,))],
+        (shape((own, cols), f32), shape((own, cols), f32), shape((own, width), f32), shape(whole, bf16)),
+        [VMEM] * (5 + len(arrived)),
+        [pltpu.VMEM((own, cols), f32)] * 2 + [pltpu.VMEM((own, cols), bf16), dma((4,))],
         (HBM,) * 4,
-    )(*near(moment, new_worker, new_server, everyone))
+    )(*near(base, begun, sent, new_server, everyone, *arrived))
     weights = call(
         functools.partial(assemble_kernel, order),
         "assemble",

time: 33.2 us -> 33.1 us (level)
  no operation moved by 1% of the time
where the time goes in v6:
time: 33.1 us; the launch traced here: 32.9 us
  blocking collectives  24.9 us (75%)
  Pallas kernels  6.23 us (19%)
  between operations  0.67 us (2%)
  starting transfers between devices  0.56 us (2%)
  waiting for transfers between devices  0.46 us (1%)
    all_to_all x2, blocking collectives, exchange(): lax.all_to_all(blocks, 'dp', split_axis=0, concat_axis=0, axis_index_grou...  24.9 us
    pallas_call x1, Pallas kernels, body(): call(gradient_kernel, 'gradient', (pltpu.VMEM((own, cols), f32), pltpu.VM...  2.38 us
    pallas_call x1, Pallas kernels, body(): call(prepare_kernel, 'prepare', (pltpu.VMEM((own, cols), f32),) * 2 + (pl...  1.29 us
    pallas_call x1, Pallas kernels, body(): call(functools.partial(keep_kernel, order), 'keep', (shape((own, cols), f...  1.15 us
    pallas_call x1, Pallas kernels, body(): call(functools.partial(assemble_kernel, order), 'assemble', shape(whole,...  0.81 us
  transfers between devices with their start and end apart: 2, of which 2 were waited for; matrix products, arithmetic and copies ran while one was open for 0% of the time, Pallas kernels for 7%

profile of v6, /device:TPU:0, one launch (start us, length us, event | category | flops | bytes accessed | tf_op | source)
XLA Modules:
  0.0 32.9 jit_solution(545798315491598672)
XLA Ops:
  0.6 2.4 %gradient.1 = (f32[8,13824]{1,0:T(8,128)S(1)}, f32[1,8,13824]{2,1,0:T(8,128)S(1)}) custom-call(bf16[16,128]{1,0:T(8,128)(2,1)} %bitcast.15, bf16[128,13824]{1,0:T(8,128)(2,1)} %bitcast.11), custom_call_target="tpu_custom_call" | custom-call | tf_op jit(solution)/shard_map/gradient/pallas_call | solution.py:208
  3.0 0.6 %collective-permute-start = (f32[8,13824]{1,0:T(8,128)S(1)}, f32[8,13824]{1,0:T(8,128)S(1)}, u32[]{:S(2)}, u32[]{:S(2)}) collective-permute-start(f32[8,13824]{1,0:T(8,128)S(1)} %bitcast.10), channel_id=1, source_target_pairs={{0,16},{16,0},{1,17},{17,1},{2,18},{18,2},{3,19},{19,3},{4,20},{20... | collective-permute-start | bytes 1327112 | tf_op jit(solution)/shard_map/ppermute | solution.py:193
  3.6 1.3 %prepare.1 = (f32[8,13824]{1,0:T(8,128)S(1)}, f32[8,13824]{1,0:T(8,128)S(1)}, f32[8,864]{1,0:T(8,128)S(1)}, f32[8,864]{1,0:T(8,128)S(1)}, f32[8,864]{1,0:T(8,128)S(1)}) custom-call(f32[8,13824]{1,0:T(8,128)} %bitcast.13, f32[8,13824]{1,0:T(8,128)} %bitcast.14, f32[8,864]{1,0:T(8,128)} %server_hbm.1, f32[8,13824]{1,0:T(8,128)} %master_hbm.1, ...), custom_call_target="tpu_custom_call" | custom-call | tf_op jit(solution)/shard_map/prepare/pallas_call | solution.py:218
  4.9 0.1 collective-permute-done.refs_0_
  5.0 0.4 %send.1 = (bf16[16,8,864]{2,1,0:T(8,128)(2,1)S(1)}, bf16[8,13824]{1,0:T(8,128)(2,1)S(1)}) custom-call(f32[8,13824]{1,0:T(8,128)S(1)} %get-tuple-element.21.start_ref, f32[8,13824]{1,0:T(8,128)S(1)} %collective-permute-done.refs_0_), custom_call_target="tpu_custom_call" | custom-call | tf_op jit(solution)/shard_map/send/pallas_call | solution.py:226
  5.4 14.2 %all_to_all.10.blocks_ref = bf16[16,8,864]{2,1,0:T(8,128)(2,1)S(1)} all-to-all(bf16[16,8,864]{2,1,0:T(8,128)(2,1)S(1)} %get-tuple-element.24), channel_id=1, replica_groups={{11,10,9,8,15,14,13,12,3,2,1,0,7,6,5,4},{27,26,25,24,31,30,29,28,19,18,..., dimensions={0} | all-to-all | bytes 442368 | tf_op jit(solution)/shard_map/all_to_all | solution.py:188
  19.6 0.2 serve.1
  19.8 10.8 %all_to_all.11.blocks_ref = bf16[16,8,864]{2,1,0:T(8,128)(2,1)S(1)} all-to-all(bf16[16,8,864]{2,1,0:T(8,128)(2,1)S(1)} %get-tuple-element.29), channel_id=1, replica_groups={{11,10,9,8,15,14,13,12,3,2,1,0,7,6,5,4},{27,26,25,24,31,30,29,28,19,18,..., dimensions={0} | all-to-all | bytes 442368 | tf_op jit(solution)/shard_map/all_to_all | solution.py:188
  30.6 0.0 collective-permute-start.1
  30.6 1.1 %keep.1 = (f32[8,13824]{1,0:T(8,128)}, f32[8,13824]{1,0:T(8,128)}, f32[8,864]{1,0:T(8,128)}, bf16[2,8,13824]{2,1,0:T(8,128)(2,1)}) custom-call(f32[8,13824]{1,0:T(8,128)S(1)} %get-tuple-element.20.base_ref, f32[8,13824]{1,0:T(8,128)S(1)} %get-tuple-element.21.start_ref, bf16[8,13824]{1,0:T(8,128)(2,1)S(1)} %get-tuple-element.23.sent_ref, ...), custom_call_target="tpu_custom_call" | custom-call | tf_op jit(solution)/shard_map/keep/pallas_call | solution.py:244
  31.7 0.3 %collective-permute-done.1.refs_0_ = bf16[16,8,864]{2,1,0:T(8,128)(2,1)S(1)} collective-permute-done((bf16[16,8,864]{2,1,0:T(8,128)(2,1)S(1)}, bf16[16,8,864]{2,1,0:T(8,128)(2,1)S(1)}, u32[]{:S(2)}, u32[]{:S(2)}) %collective-permute-start.1) | collective-permute-done | bytes 221216 | tf_op jit(solution)/shard_map/ppermute | solution.py:193
  32.0 0.8 %assemble.1 = bf16[2,8,13824]{2,1,0:T(8,128)(2,1)} custom-call(bf16[16,8,864]{2,1,0:T(8,128)(2,1)S(1)} %collective-permute-done.1.refs_0_, bf16[2,8,13824]{2,1,0:T(8,128)(2,1)} %get-tuple-element.33.refs_1_), custom_call_target="tpu_custom_call", output_to_operand_aliasing={{}: (1, {})} | custom-call | tf_op jit(solution)/shard_map/assemble/pallas_call | solution.py:252
Async XLA Ops:
  3.0 2.0 %collective-permute-start = (f32[8,13824]{1,0:T(8,128)S(1)}, f32[8,13824]{1,0:T(8,128)S(1)}, u32[]{:S(2)}, u32[]{:S(2)}) collective-permute-start(f32[8,13824]{1,0:T(8,128)S(1)} %bitcast.10), channel_id=1, source_target_pairs={{0,16},{16,0},{1,17},{17,1},{2,18},{18,2},{3,19},{19,3},{4,20},{20... | collective-permute-start | bytes 1327112 | tf_op jit(solution)/shard_map/ppermute | solution.py:193
  30.6 1.5 %collective-permute-start.1 = (bf16[16,8,864]{2,1,0:T(8,128)(2,1)S(1)}, bf16[16,8,864]{2,1,0:T(8,128)(2,1)S(1)}, u32[]{:S(2)}, u32[]{:S(2)}) collective-permute-start(bf16[16,8,864]{2,1,0:T(8,128)(2,1)S(1)} %all_to_all.11.blocks_ref), channel_id=1, source_target_pairs={{0,16},{16,0},{1,17},{17,1},{2,18},{18,2},{3,19},{19,3},{4,20},{20... | collective-permute-start | bytes 663560 | tf_op jit(solution)/shard_map/ppermute | solution.py:193

commit v7 on v6

--- a/solution.py
+++ b/solution.py
@@ -171,9 +171,13 @@
         copy.wait()
 
 
-def ordered(count):
+def ordered(count, turned=False):
     lead = count // 2 + count // 4 - 1
-    return [lead ^ i if count & (count - 1) == 0 else (lead - i) % count for i in range(count)]
+    if count & (count - 1):
+        return [(lead - i) % count for i in range(count)]
+    bits = count.bit_length() - 1
+    places = [sum((i >> k & 1) << (bits - 1 - k) for k in range(bits)) if turned else i for i in range(count)]
+    return [lead ^ place for place in places]
 
 
 def body(hidden, cotangent, momentum, worker_error, server_error, master, second_moment):
@@ -184,10 +188,10 @@
     width = cols // servers
     shape = jax.ShapeDtypeStruct
 
-    def exchange(blocks):
+    def exchange(blocks, order):
         return lax.all_to_all(blocks, "dp", split_axis=0, concat_axis=0, axis_index_groups=[order], tiled=True)
 
-    order = ordered(servers)
+    first, order = ordered(servers, True), ordered(servers)
 
     def turn(value, k):
         return lax.ppermute(value, "node", [(i, (i + k) % nodes) for i in range(nodes)])
@@ -224,12 +228,12 @@
     )(*far(momentum[0], worker_error[0], server_error, master, second_moment), *near(mine))
 
     blocks, sent = call(
-        functools.partial(send_kernel, order),
+        functools.partial(send_kernel, first),
         "send",
         (pltpu.VMEM((servers, own, width), bf16), pltpu.VMEM((own, cols), bf16)),
         [VMEM] * (1 + len(arrived)),
     )(*near(begun, *arrived))
-    gathered = exchange(blocks)
+    gathered = exchange(blocks, first)
 
     new_server, copies = call(
         serve_kernel,
@@ -237,7 +241,7 @@
         (pltpu.VMEM((own, width), f32), pltpu.VMEM((servers, own, width), bf16)),
         [VMEM] * 4,
     )(*near(gathered, server, master_part, bottom))
-    everyone = exchange(copies)
+    everyone = exchange(copies, order)
     others = [turn(everyone, k) for k in range(1, nodes)]
 
     whole = (nodes, own, cols)

time: 33.1 us -> 33.1 us (level)
  no operation moved by 1% of the time
where the time goes in v7:
time: 33.1 us; the launch traced here: 32.9 us
  blocking collectives  25 us (76%)
  Pallas kernels  6.23 us (19%)
  between operations  0.67 us (2%)
  starting transfers between devices  0.56 us (2%)
  waiting for transfers between devices  0.46 us (1%)
    all_to_all x2, blocking collectives, exchange(): lax.all_to_all(blocks, 'dp', split_axis=0, concat_axis=0, axis_index_grou...  25 us
    pallas_call x1, Pallas kernels, body(): call(gradient_kernel, 'gradient', (pltpu.VMEM((own, cols), f32), pltpu.VM...  2.38 us
    pallas_call x1, Pallas kernels, body(): call(prepare_kernel, 'prepare', (pltpu.VMEM((own, cols), f32),) * 2 + (pl...  1.29 us
    pallas_call x1, Pallas kernels, body(): call(functools.partial(keep_kernel, order), 'keep', (shape((own, cols), f...  1.15 us
    pallas_call x1, Pallas kernels, body(): call(functools.partial(assemble_kernel, order), 'assemble', shape(whole,...  0.81 us
  transfers between devices with their start and end apart: 2, of which 2 were waited for; matrix products, arithmetic and copies ran while one was open for 0% of the time, Pallas kernels for 7%

profile of v7, /device:TPU:0, one launch (start us, length us, event | category | flops | bytes accessed | tf_op | source)
XLA Modules:
  0.0 32.9 jit_solution(17019684220885126485)
XLA Ops:
  0.6 2.4 %gradient.1 = (f32[8,13824]{1,0:T(8,128)S(1)}, f32[1,8,13824]{2,1,0:T(8,128)S(1)}) custom-call(bf16[16,128]{1,0:T(8,128)(2,1)} %bitcast.15, bf16[128,13824]{1,0:T(8,128)(2,1)} %bitcast.11), custom_call_target="tpu_custom_call" | custom-call | tf_op jit(solution)/shard_map/gradient/pallas_call | solution.py:212
  3.0 0.6 %collective-permute-start = (f32[8,13824]{1,0:T(8,128)S(1)}, f32[8,13824]{1,0:T(8,128)S(1)}, u32[]{:S(2)}, u32[]{:S(2)}) collective-permute-start(f32[8,13824]{1,0:T(8,128)S(1)} %bitcast.10), channel_id=1, source_target_pairs={{0,16},{16,0},{1,17},{17,1},{2,18},{18,2},{3,19},{19,3},{4,20},{20... | collective-permute-start | bytes 1327112 | tf_op jit(solution)/shard_map/ppermute | solution.py:197
  3.6 1.3 %prepare.1 = (f32[8,13824]{1,0:T(8,128)S(1)}, f32[8,13824]{1,0:T(8,128)S(1)}, f32[8,864]{1,0:T(8,128)S(1)}, f32[8,864]{1,0:T(8,128)S(1)}, f32[8,864]{1,0:T(8,128)S(1)}) custom-call(f32[8,13824]{1,0:T(8,128)} %bitcast.13, f32[8,13824]{1,0:T(8,128)} %bitcast.14, f32[8,864]{1,0:T(8,128)} %server_hbm.1, f32[8,13824]{1,0:T(8,128)} %master_hbm.1, ...), custom_call_target="tpu_custom_call" | custom-call | tf_op jit(solution)/shard_map/prepare/pallas_call | solution.py:222
  4.9 0.1 collective-permute-done.refs_0_
  5.0 0.4 %send.1 = (bf16[16,8,864]{2,1,0:T(8,128)(2,1)S(1)}, bf16[8,13824]{1,0:T(8,128)(2,1)S(1)}) custom-call(f32[8,13824]{1,0:T(8,128)S(1)} %get-tuple-element.21.start_ref, f32[8,13824]{1,0:T(8,128)S(1)} %collective-permute-done.refs_0_), custom_call_target="tpu_custom_call" | custom-call | tf_op jit(solution)/shard_map/send/pallas_call | solution.py:230
  5.4 14.4 %all_to_all.10.blocks_ref = bf16[16,8,864]{2,1,0:T(8,128)(2,1)S(1)} all-to-all(bf16[16,8,864]{2,1,0:T(8,128)(2,1)S(1)} %get-tuple-element.24), channel_id=1, replica_groups={{11,3,15,7,9,1,13,5,10,2,14,6,8,0,12,4},{27,19,31,23,25,17,29,21,26,18,..., dimensions={0} | all-to-all | bytes 442368 | tf_op jit(solution)/shard_map/all_to_all | solution.py:192
  19.8 0.2 serve.1
  20.0 10.6 %all_to_all.11.blocks_ref = bf16[16,8,864]{2,1,0:T(8,128)(2,1)S(1)} all-to-all(bf16[16,8,864]{2,1,0:T(8,128)(2,1)S(1)} %get-tuple-element.29), channel_id=1, replica_groups={{11,10,9,8,15,14,13,12,3,2,1,0,7,6,5,4},{27,26,25,24,31,30,29,28,19,18,..., dimensions={0} | all-to-all | bytes 442368 | tf_op jit(solution)/shard_map/all_to_all | solution.py:192
  30.6 0.0 collective-permute-start.1
  30.6 1.1 %keep.1 = (f32[8,13824]{1,0:T(8,128)}, f32[8,13824]{1,0:T(8,128)}, f32[8,864]{1,0:T(8,128)}, bf16[2,8,13824]{2,1,0:T(8,128)(2,1)}) custom-call(f32[8,13824]{1,0:T(8,128)S(1)} %get-tuple-element.20.base_ref, f32[8,13824]{1,0:T(8,128)S(1)} %get-tuple-element.21.start_ref, bf16[8,13824]{1,0:T(8,128)(2,1)S(1)} %get-tuple-element.23.sent_ref, ...), custom_call_target="tpu_custom_call" | custom-call | tf_op jit(solution)/shard_map/keep/pallas_call | solution.py:248
  31.7 0.3 %collective-permute-done.1.refs_0_ = bf16[16,8,864]{2,1,0:T(8,128)(2,1)S(1)} collective-permute-done((bf16[16,8,864]{2,1,0:T(8,128)(2,1)S(1)}, bf16[16,8,864]{2,1,0:T(8,128)(2,1)S(1)}, u32[]{:S(2)}, u32[]{:S(2)}) %collective-permute-start.1) | collective-permute-done | bytes 221216 | tf_op jit(solution)/shard_map/ppermute | solution.py:197
  32.1 0.8 %assemble.1 = bf16[2,8,13824]{2,1,0:T(8,128)(2,1)} custom-call(bf16[16,8,864]{2,1,0:T(8,128)(2,1)S(1)} %collective-permute-done.1.refs_0_, bf16[2,8,13824]{2,1,0:T(8,128)(2,1)} %get-tuple-element.33.refs_1_), custom_call_target="tpu_custom_call", output_to_operand_aliasing={{}: (1, {})} | custom-call | tf_op jit(solution)/shard_map/assemble/pallas_call | solution.py:256
Async XLA Ops:
  3.0 2.0 %collective-permute-start = (f32[8,13824]{1,0:T(8,128)S(1)}, f32[8,13824]{1,0:T(8,128)S(1)}, u32[]{:S(2)}, u32[]{:S(2)}) collective-permute-start(f32[8,13824]{1,0:T(8,128)S(1)} %bitcast.10), channel_id=1, source_target_pairs={{0,16},{16,0},{1,17},{17,1},{2,18},{18,2},{3,19},{19,3},{4,20},{20... | collective-permute-start | bytes 1327112 | tf_op jit(solution)/shard_map/ppermute | solution.py:197
  30.6 1.5 %collective-permute-start.1 = (bf16[16,8,864]{2,1,0:T(8,128)(2,1)S(1)}, bf16[16,8,864]{2,1,0:T(8,128)(2,1)S(1)}, u32[]{:S(2)}, u32[]{:S(2)}) collective-permute-start(bf16[16,8,864]{2,1,0:T(8,128)(2,1)S(1)} %all_to_all.11.blocks_ref), channel_id=1, source_target_pairs={{0,16},{16,0},{1,17},{17,1},{2,18},{18,2},{3,19},{19,3},{4,20},{20... | collective-permute-start | bytes 663560 | tf_op jit(solution)/shard_map/ppermute | solution.py:197
